TPU v7x, 256 devices: a whole 4x4x8 slice. The times are simulated.
256 devices in a mesh: row: 16 (over y, x), col: 2 (over core), ctx: 8 (over z).
Axes of the slice: x: 4, y: 4, z: 8, core: 2. Of those that a mesh axis runs over, the one named last changes fastest.
Arguments:
- queries: bfloat16 [8192, 6144], P(('col', 'ctx'), 'row'), may hold values from -16 to 16
- keys: bfloat16 [8192, 6144], P(('col', 'ctx'), 'row'), may hold values from -16 to 16
- values: bfloat16 [8192, 6144], P(('col', 'ctx'), 'row'), may hold values from -6 to 6
- out_weight: bfloat16 [6144, 6144], P('col', 'row'), may hold values from -0.078125 to 0.078125
- cotangent: bfloat16 [8192, 6144], P(('col', 'ctx'), 'row'), may hold values from -0.125 to 0.125
- block_mask: int32 [16, 16], replicated, may hold values from 0 to 1, as said below
Outputs:
- mixed_out: bfloat16 [8192, 6144], P(('col', 'ctx'), 'row')
- grad_weight: bfloat16 [6144, 6144], P(('col', 'ctx'), 'row')
Inputs may be any that keep to these rules, and one draw needn't show every extreme that they name: block_mask[i, i] is 1 for every block i, and block_mask[i, j] is 0 for j > i.
All inputs are finite; a program needn't handle non-finite values.
Results may differ from a plain program's by a relative error of at most 0.013.
Values may be sent and summed in bfloat16 or wider, within the bound.
A program may use at most 64 MiB of HBM per device.

v0:
```python
import math

import jax
import jax.numpy as jnp
from jax import lax
from jax.sharding import PartitionSpec as P

HD = 128
BLOCK = 512


NEGATIVE_FILL = -1e30


def attend_block(carried, query_heads, key_block, value_block, allowed, score_scale):
    run_max, run_sum, weighted = carried
    tok_rows, head_count, head_size = query_heads.shape
    key_heads = key_block.reshape(key_block.shape[0], head_count, head_size)
    value_heads = value_block.reshape(value_block.shape[0], head_count, head_size)
    scores = (
        jnp.einsum("thd,uhd->thu", query_heads, key_heads, preferred_element_type=jnp.float32)
        * score_scale
    )
    scores = jnp.where(allowed[:, None, None], scores, NEGATIVE_FILL)
    new_max = jnp.maximum(run_max, jnp.max(scores, axis=2))
    correction = jnp.exp(run_max - new_max)
    weights = jnp.where(allowed[:, None, None], jnp.exp(scores - new_max[:, :, None]), 0.0)
    new_sum = run_sum * correction + jnp.sum(weights, axis=2)
    product = jnp.einsum(
        "thu,uhd->thd",
        weights.astype(jnp.bfloat16),
        value_heads,
        preferred_element_type=jnp.float32,
    )
    new_weighted = weighted * correction[:, :, None] + product
    return (new_max, new_sum, new_weighted)


def body(queries, keys, values, out_weight, cotangent, block_mask):
    tok_rows, feature_width = queries.shape
    head_count = feature_width // HD
    query_heads = queries.reshape(tok_rows, head_count, HD)
    score_scale = 1.0 / math.sqrt(HD)
    local_blocks = tok_rows // BLOCK
    first_block = lax.axis_index(("col", "ctx")) * local_blocks
    local_mask = lax.dynamic_slice_in_dim(block_mask, first_block, local_blocks, 0)
    start_state = (
        jnp.full((tok_rows, head_count), NEGATIVE_FILL, jnp.float32),
        jnp.zeros((tok_rows, head_count), jnp.float32),
        jnp.zeros((tok_rows, head_count, HD), jnp.float32),
    )
    key_piece = lax.all_gather(keys, ("col", "ctx"), axis=0, tiled=True)
    value_piece = lax.all_gather(values, ("col", "ctx"), axis=0, tiled=True)
    block_count = key_piece.shape[0] // BLOCK
    key_stack = key_piece.reshape(block_count, BLOCK, feature_width)
    value_stack = value_piece.reshape(block_count, BLOCK, feature_width)
    block_columns = jnp.arange(block_count, dtype=jnp.int32)

    def one_block(state_in, entries):
        key_block, value_block, block_column = entries
        mask_column = lax.dynamic_index_in_dim(local_mask, block_column, 1, keepdims=False)
        allowed = jnp.repeat(mask_column, BLOCK, total_repeat_length=tok_rows) == 1
        updated = attend_block(state_in, query_heads, key_block, value_block, allowed, score_scale)
        return (updated, None)

    state_out, _ = lax.scan(one_block, start_state, (key_stack, value_stack, block_columns))
    run_max, run_sum, weighted = state_out
    attended = (
        (weighted / run_sum[:, :, None]).reshape(tok_rows, feature_width).astype(jnp.bfloat16)
    )
    all_heads = lax.all_gather(attended, "row", axis=1, tiled=True)
    head_columns = all_heads
    mixed_out = jnp.dot(
        head_columns,
        lax.all_gather(out_weight, "col", axis=0, tiled=True),
        preferred_element_type=jnp.float32,
    )
    head_columns = all_heads
    grad_weight = lax.psum_scatter(
        lax.dot_general(
            head_columns, cotangent, (((0,), (0,)), ((), ())), preferred_element_type=jnp.float32
        ),
        ("col", "ctx"),
        scatter_dimension=0,
        tiled=True,
    )
    return (mixed_out.astype(jnp.bfloat16), grad_weight.astype(jnp.bfloat16))


def solution(mesh):
    in_specs = (
        P(("col", "ctx"), "row"),
        P(("col", "ctx"), "row"),
        P(("col", "ctx"), "row"),
        P("col", "row"),
        P(("col", "ctx"), "row"),
        P(),
    )
    out_specs = (P(("col", "ctx"), "row"), P(("col", "ctx"), "row"))
    return jax.shard_map(body, mesh=mesh, in_specs=in_specs, out_specs=out_specs, check_vma=False)
```

profile of v0, /device:TPU:1, one launch (start us, length us, event | category | flops | bytes accessed | tf_op | source)
XLA Modules:
  0.0 622.6 jit_solution(9049366893125646251)
XLA Ops:
  12.0 48.1 %all-gather.5.cloned.1.call-done = bf16[8192,384]{1,0:T(8,128)(2,1)} async-done(((bf16[512,384]{1,0:T(8,128)(2,1)}), bf16[8192,384]{1,0:T(8,128)(2,1)}) %all-gather.5.cloned.1.call-update) | async-done | bytes 6291472 | tf_op jit(solution)/shard_map/all_gather | solution.py:52
  60.1 46.5 %all-gather.7.cloned.1.call-done = bf16[8192,384]{1,0:T(8,128)(2,1)} async-done(((bf16[512,384]{1,0:T(8,128)(2,1)}), bf16[8192,384]{1,0:T(8,128)(2,1)}) %all-gather.7.cloned.1.call-update) | async-done | bytes 6291472 | tf_op jit(solution)/shard_map/all_gather | solution.py:53
  107.2 304.6 %while.22 = (s32[]{:T(128)}, f32[512,3]{0,1:T(4,128)}, f32[512,3]{0,1:T(4,128)}, f32[512,3,128]{0,2,1:T(8,128)}, s32[16]{0:T(128)}, /*index=5*/s32[1,16]{1,0:T(1...) while((s32[]{:T(128)}, f32[512,3]{0,1:T(4,128)}, ...), condition=%wide.region_3.4_spmd.clone, body=%wide.region_0.3_spmd.clone.sunk | while | flops 413474304 | bytes 15433919 | solution.py:66
  120.7 3.4 fusion.42
  139.5 3.7 fusion.42
  158.7 3.7 fusion.42
  177.8 3.7 fusion.42
  197.0 3.7 fusion.42
  216.1 3.7 fusion.42
  235.2 3.7 fusion.42
  254.4 3.7 fusion.42
  273.5 3.7 fusion.42
  292.7 3.7 fusion.42
  311.8 3.7 fusion.42
  330.9 3.7 fusion.42
  350.1 3.7 fusion.42
  369.2 3.7 fusion.42
  388.3 3.7 fusion.42
  407.5 3.7 fusion.42
  414.4 64.1 %all-gather.9.cloned.1.call-done = bf16[512,6144]{0,1:T(8,128)(2,1)} async-done(((bf16[512,384]{0,1:T(8,128)(2,1)}), bf16[512,6144]{0,1:T(8,128)(2,1)}) %all-gather.9.cloned.1.call-update) | async-done | bytes 6291472 | tf_op jit(solution)/shard_map/all_gather | solution.py:71
  478.5 9.9 %fusion.19 = f32[6144,384]{1,0:T(8,128)} fusion(bf16[512,6144]{0,1:T(8,128)(2,1)} %all-gather.9.cloned.1.call-done, bf16[512,384]{1,0:T(8,128)(2,1)S(1)} %copy-done), kind=kOutput, calls=%fused_computation.27 | convolution fusion | flops 2415919104 | bytes 16121856 | tf_op jit(solution)/shard_map/dot_general | solution.py:80
  488.4 12.0 %all-gather.11.cloned.1.call-done = bf16[6144,384]{1,0:T(8,128)(2,1)} async-done(((bf16[3072,384]{1,0:T(8,128)(2,1)}), bf16[6144,384]{1,0:T(8,128)(2,1)}) %all-gather.11.cloned.1.call-update) | async-done | bytes 4718608 | tf_op jit(solution)/shard_map/all_gather | solution.py:75
  500.4 8.3 %convolution_convert_fusion = bf16[512,384]{1,0:T(8,128)(2,1)} fusion(bf16[512,6144]{0,1:T(8,128)(2,1)} %all-gather.9.cloned.1.call-done, bf16[6144,384]{1,0:T(8,128)(2,1)} %all-gather.11.cloned.1.call-done), kind=kOutput, calls=%fused_computation.23 | convolution fusion | flops 2416115712 | bytes 11403264 | tf_op jit(solution)/shard_map/dot_general | solution.py:73
  508.7 105.5 %reduce-scatter.2.cloned.1.call-done = f32[384,384]{1,0:T(8,128)} async-done(((f32[6144,384]{1,0:T(8,128)}), f32[384,384]{1,0:T(8,128)}) %reduce-scatter.2.cloned.1.call-update) | async-done | bytes 589840 | tf_op jit(solution)/shard_map/reduce_scatter | solution.py:79
  (181 shorter events, 226.0 us)
Async XLA Ops:
  7.2 471.3 %copy-start = (bf16[512,384]{1,0:T(8,128)(2,1)S(1)}, bf16[512,384]{1,0:T(8,128)(2,1)}, u32[]{:S(2)}) copy-start(bf16[512,384]{1,0:T(8,128)(2,1)} %param.16) | copy-start | bytes 1179652
  7.2 53.0 %all-gather.5.cloned.1.call-start = ((), (), s32[]{:S(2)}) async-start(), calls=%async_computation.1 | async-start | bytes 6684672 | tf_op jit(solution)/shard_map/all_gather | solution.py:52
  7.9 98.7 %all-gather.7.cloned.1.call-start = ((), (), s32[]{:S(2)}) async-start(), calls=%async_computation.2 | async-start | bytes 6684672 | tf_op jit(solution)/shard_map/all_gather | solution.py:53
  8.7 469.8 %all-gather.9.cloned.1.call-start = ((), (), s32[]{:S(2)}) async-start(), calls=%async_computation.3 | async-start | bytes 6684672 | tf_op jit(solution)/shard_map/all_gather | solution.py:71
  413.7 86.7 %all-gather.11.cloned.1.call-start = ((), (), s32[]{:S(2)}) async-start(), calls=%async_computation.4 | async-start | bytes 7077888 | tf_op jit(solution)/shard_map/all_gather | solution.py:75
  414.3 200.0 %reduce-scatter.2.cloned.1.call-start = ((), (), s32[]{:S(2)}) async-start(), calls=%async_computation.5 | async-start | bytes 10027008 | tf_op jit(solution)/shard_map/reduce_scatter | solution.py:79
Sparse Core Ops, SparseCore 0:
  9.8 50.2 all-gather.4
  62.0 44.6 all-gather.6
  413.9 64.5 all-gather.8
  480.1 20.2 all-gather.10
  502.8 111.4 reduce-scatter.1
where the time goes:
time: 627 us; the launch traced here: 623 us
  waiting for transfers between devices  278 us (44%)
  matrix products  115 us (18%)
  local copies, waits for them, and re-layouts  110 us (18%)
  other arithmetic  75.8 us (12%)
  loops' own time  29.9 us (5%)
  between operations  13.8 us (2%)
    reduce_scatter x1, waiting for transfers between devices, body(): lax.psum_scatter(lax.dot_general(head_columns, cotangent, (((0,), (0,)),...  106 us
    dynamic_slice x64, local copies, waits for them, and re-layouts, body(): lax.scan(one_block, start_state, (key_stack, value_stack, block_columns))  96.5 us
    all_gather x1, waiting for transfers between devices, body(): all_heads = lax.all_gather(attended, 'row', axis=1, tiled=True)  64.1 us
    dot_general x16, matrix products, attend_block(): jnp.einsum('thu,uhd->thd', weights.astype(jnp.bfloat16), value_heads, pre...  58.4 us
    all_gather x1, waiting for transfers between devices, body(): key_piece = lax.all_gather(keys, ('col', 'ctx'), axis=0, tiled=True)  48.1 us
    all_gather x1, waiting for transfers between devices, body(): value_piece = lax.all_gather(values, ('col', 'ctx'), axis=0, tiled=True)  46.5 us
    dot_general x16, matrix products, attend_block(): jnp.einsum('thd,uhd->thu', query_heads, key_heads, preferred_element_type...  38.2 us
    another operation x1, loops' own time, body(): lax.scan(one_block, start_state, (key_stack, value_stack, block_columns))  29.9 us
  transfers between devices with their start and end apart: 5, of which 5 were waited for; matrix products, arithmetic and copies ran while one was open for 3% of the time, Pallas kernels for 0%

commit v1 on v0

v1 whole, which is shorter than its diff:
```python
import functools
import math

import jax
import jax.numpy as jnp
from jax import lax
from jax.experimental import pallas as pl
from jax.experimental.pallas import tpu as pltpu
from jax.sharding import PartitionSpec as P

HD = 128
BLOCK = 512


def attend_kernel(place_ref, mask_ref, q_ref, k_ref, v_ref, out_ref, run_max, run_sum, weighted):
    back = pl.program_id(1)
    block = place_ref[0] - back
    rate = math.log2(math.e) / math.sqrt(HD)

    @pl.when(back == 0)
    def _():
        run_max[...] = jnp.full_like(run_max, -1e30)
        run_sum[...] = jnp.zeros_like(run_sum)
        weighted[...] = jnp.zeros_like(weighted)

    @pl.when((block >= 0) & (mask_ref[jnp.maximum(block, 0)] == 1))
    def _():
        scores = lax.dot_general(
            q_ref[...], k_ref[...], (((1,), (1,)), ((), ())), preferred_element_type=jnp.float32
        )
        new_max = jnp.maximum(run_max[...], jnp.max(scores, axis=1, keepdims=True))
        correction = jnp.exp2((run_max[...] - new_max) * rate)
        weights = jnp.exp2((scores - new_max) * rate)
        run_sum[...] = run_sum[...] * correction + jnp.sum(weights, axis=1, keepdims=True)
        weighted[...] = weighted[...] * correction + jnp.dot(
            weights.astype(jnp.bfloat16), v_ref[...], preferred_element_type=jnp.float32
        )
        run_max[...] = new_max

    @pl.when(back == pl.num_programs(1) - 1)
    def _():
        out_ref[...] = (weighted[...] / run_sum[...]).astype(out_ref.dtype)


def attend(place, mask_row, queries, keys, values):
    rows, width = queries.shape
    blocks = keys.shape[0] // BLOCK
    heads = width // HD
    kv_spec = pl.BlockSpec((BLOCK, HD), lambda h, b, place, mask: (jnp.maximum(place[0] - b, 0), h))
    q_spec = pl.BlockSpec((BLOCK, HD), lambda h, b, place, mask: (0, h))
    return pl.pallas_call(
        attend_kernel,
        out_shape=jax.ShapeDtypeStruct((rows, width), jnp.bfloat16),
        grid_spec=pltpu.PrefetchScalarGridSpec(
            num_scalar_prefetch=2,
            grid=(heads, blocks),
            in_specs=[q_spec, kv_spec, kv_spec],
            out_specs=q_spec,
            scratch_shapes=[
                pltpu.VMEM((rows, 1), jnp.float32),
                pltpu.VMEM((rows, 1), jnp.float32),
                pltpu.VMEM((rows, HD), jnp.float32),
            ],
        ),
        compiler_params=pltpu.CompilerParams(
            dimension_semantics=("arbitrary", "arbitrary"), vmem_limit_bytes=32 << 20
        ),
    )(place, mask_row, queries, keys, values)


def body(queries, keys, values, out_weight, cotangent, block_mask):
    place = lax.axis_index(("col", "ctx"))
    mask_row = lax.dynamic_index_in_dim(block_mask, place, 0, keepdims=False)
    all_keys = lax.all_gather(keys, ("col", "ctx"), axis=0, tiled=True)
    all_values = lax.all_gather(values, ("col", "ctx"), axis=0, tiled=True)
    weight = lax.all_gather(out_weight, "col", axis=0, tiled=True)
    attended = attend(place.reshape(1), mask_row, queries, all_keys, all_values)
    all_heads = lax.all_gather(attended, "row", axis=1, tiled=True)
    partial = lax.dot_general(
        all_heads, cotangent, (((0,), (0,)), ((), ())), preferred_element_type=jnp.float32
    ).astype(jnp.bfloat16)
    grad_weight = lax.psum_scatter(partial, ("col", "ctx"), scatter_dimension=0, tiled=True)
    mixed_out = jnp.dot(all_heads, weight, preferred_element_type=jnp.float32)
    return (mixed_out.astype(jnp.bfloat16), grad_weight)


def solution(mesh):
    tokens = P(("col", "ctx"), "row")
    return jax.shard_map(
        body,
        mesh=mesh,
        in_specs=(tokens, tokens, tokens, P("col", "row"), tokens, P()),
        out_specs=(tokens, tokens),
        check_vma=False,
    )
```

time: 627 us -> 331 us (0.53)
  local copies, waits for them, and re-layouts: 110 us -> 7.27 us
  matrix products: 115 us -> 16.8 us
  other arithmetic: 75.8 us -> 0 us
  loops' own time: 29.9 us -> 0 us
  Pallas kernels: 0 us -> 25.2 us
  waiting for transfers between devices: 278 us -> 268 us
    dot_general x34 -> x2, matrix products: 115 us -> 16.8 us  [the longest x1 8.46 us: body(): lax.dot_general(all_heads, cotangent, (((0,), (0,)), ((), ())), preferred...]
    dynamic_slice x65 -> x0, local copies, waits for them, and re-layouts: 97.7 us -> none  [the longest x64 96.5 us: body(): lax.scan(one_block, start_state, (key_stack, value_stack, block_columns))]
    reduce_scatter x1, waiting for transfers between devices: 106 us -> 69.9 us  [body(): lax.psum_scatter(partial, ('col', 'ctx'), scatter_dimension=0, tiled=True)]
    another operation x1 -> x0, loops' own time: 29.9 us -> none  [body(): lax.scan(one_block, start_state, (key_stack, value_stack, block_columns))]
    pallas_call x0 -> x1, Pallas kernels: none -> 25.2 us  [attend(): pl.pallas_call(attend_kernel, out_shape=jax.ShapeDtypeStruct((rows, width...]
    reduce_sum x16 -> x0, other arithmetic: 21.6 us -> none  [attend_block(): new_sum = run_sum * correction + jnp.sum(weights, axis=2)]
    all_gather x1, waiting for transfers between devices: 64.1 us -> 84.7 us  [body(): all_heads = lax.all_gather(attended, 'row', axis=1, tiled=True)]
    add x16 -> x0, other arithmetic: 20.6 us -> none  [attend_block(): new_sum = run_sum * correction + jnp.sum(weights, axis=2)]
  transfers between devices with their start and end apart: 5 -> 5, of which waited for: 5 -> 5; matrix products, arithmetic and copies ran while one was open for 3% -> 5% of each run, Pallas kernels for 0% -> 0%
where the time goes in v1:
time: 331 us
  waiting for transfers between devices  268 us (81%)
  Pallas kernels  25.2 us (8%)
  matrix products  16.8 us (5%)
  between operations  13.8 us (4%)
  local copies, waits for them, and re-layouts  7.27 us (2%)
    all_gather x1, waiting for transfers between devices, body(): all_heads = lax.all_gather(attended, 'row', axis=1, tiled=True)  84.7 us
    reduce_scatter x1, waiting for transfers between devices, body(): lax.psum_scatter(partial, ('col', 'ctx'), scatter_dimension=0, tiled=True)  69.9 us
    all_gather x1, waiting for transfers between devices, body(): all_keys = lax.all_gather(keys, ('col', 'ctx'), axis=0, tiled=True)  50.7 us
    all_gather x1, waiting for transfers between devices, body(): all_values = lax.all_gather(values, ('col', 'ctx'), axis=0, tiled=True)  46.5 us
    pallas_call x1, Pallas kernels, attend(): pl.pallas_call(attend_kernel, out_shape=jax.ShapeDtypeStruct((rows, width...  25.2 us
    all_gather x1, waiting for transfers between devices, body(): weight = lax.all_gather(out_weight, 'col', axis=0, tiled=True)  14 us
    dot_general x1, matrix products, body(): lax.dot_general(all_heads, cotangent, (((0,), (0,)), ((), ())), preferred...  8.46 us
    dot_general x1, matrix products, body(): mixed_out = jnp.dot(all_heads, weight, preferred_element_type=jnp.float32)  8.31 us
  transfers between devices with their start and end apart: 5, of which 5 were waited for; matrix products, arithmetic and copies ran while one was open for 5% of the time, Pallas kernels for 0%

profile of v1, /device:TPU:1, one launch (start us, length us, event | category | flops | bytes accessed | tf_op | source)
XLA Modules:
  0.0 331.1 jit_solution(16592447865117818077)
XLA Ops:
  7.2 0.0 copy-start
  7.2 0.0 all-gather.5.cloned.1.call-start
  7.2 0.7 all-gather.5.cloned.1.call-update
  7.9 0.0 all-gather.7.cloned.1.call-start
  8.0 0.7 all-gather.7.cloned.1.call-update
  8.7 0.0 all-gather.9.cloned.1.call-start
  8.7 0.7 dynamic-slice_bitcast_fusion.mask_ref
  9.4 50.7 %all-gather.5.cloned.1.call-done.k_ref = bf16[8192,384]{1,0:T(8,128)(2,1)} async-done(((bf16[512,384]{1,0:T(8,128)(2,1)}), bf16[8192,384]{1,0:T(8,128)(2,1)}) %all-gather.5.cloned.1.call-update) | async-done | bytes 6291472 | tf_op jit(solution)/shard_map/all_gather | solution.py:74
  60.1 46.5 %all-gather.7.cloned.1.call-done.v_ref = bf16[8192,384]{1,0:T(8,128)(2,1)} async-done(((bf16[512,384]{1,0:T(8,128)(2,1)}), bf16[8192,384]{1,0:T(8,128)(2,1)}) %all-gather.7.cloned.1.call-update) | async-done | bytes 6291472 | tf_op jit(solution)/shard_map/all_gather | solution.py:75
  106.7 2.8 copy-done.1
  109.4 2.8 copy-done.2
  112.2 1.0 copy-done.3
  113.2 25.2 %shard_map.77 = bf16[512,384]{1,0:T(8,128)(2,1)} custom-call(s32[1]{0:T(128)} %bitcast.place_ref, s32[16]{0:T(128)S(1)} %dynamic-slice_bitcast_fusion.mask_ref, bf16[512,384]{1,0:T(8,128)(2,1)S(1)} %copy-done.3, bf16[8192,384]{1,0:T(8,128)(2,1)S(1)} %copy-done.1, bf16[8192,384]{1,0:T(8,128)(2,1)S(1)} %copy-done.2), custom_call_target="tpu_custom_call" | custom-call | tf_op jit(solution)/shard_map/pallas_call | solution.py:51
  138.4 0.0 all-gather.9.cloned.1.call-update
  138.4 0.0 all-gather.11.cloned.1.call-start
  138.5 0.5 all-gather.11.cloned.1.call-update
  139.0 0.0 reduce-scatter.2.cloned.1.call-start
  139.1 84.7 %all-gather.9.cloned.1.call-done = bf16[512,6144]{1,0:T(8,128)(2,1)} async-done(((bf16[512,384]{1,0:T(8,128)(2,1)}), bf16[512,6144]{1,0:T(8,128)(2,1)}) %all-gather.9.cloned.1.call-update) | async-done | bytes 6291472 | tf_op jit(solution)/shard_map/all_gather | solution.py:78
  223.8 0.0 copy-done
  223.8 8.5 %convolution_convert_fusion = bf16[6144,384]{1,0:T(8,128)(2,1)} fusion(bf16[512,6144]{1,0:T(8,128)(2,1)} %all-gather.9.cloned.1.call-done, bf16[512,384]{1,0:T(8,128)(2,1)S(1)} %copy-done), kind=kOutput, calls=%fused_computation | convolution fusion | flops 2418278400 | bytes 11403264 | tf_op jit(solution)/shard_map/dot_general | solution.py:79
  232.3 0.0 reduce-scatter.2.cloned.1.call-update
  232.3 14.0 %all-gather.11.cloned.1.call-done = bf16[6144,384]{1,0:T(8,128)(2,1)} async-done(((bf16[3072,384]{1,0:T(8,128)(2,1)}), bf16[6144,384]{1,0:T(8,128)(2,1)}) %all-gather.11.cloned.1.call-update) | async-done | bytes 4718608 | tf_op jit(solution)/shard_map/all_gather | solution.py:76
  246.3 8.3 %convolution_convert_fusion.1 = bf16[512,384]{1,0:T(8,128)(2,1)} fusion(bf16[512,6144]{1,0:T(8,128)(2,1)} %all-gather.9.cloned.1.call-done, bf16[6144,384]{1,0:T(8,128)(2,1)} %all-gather.11.cloned.1.call-done), kind=kOutput, calls=%fused_computation.1 | convolution fusion | flops 2416115712 | bytes 11403264 | tf_op jit(solution)/shard_map/dot_general | solution.py:83
  254.6 69.9 %reduce-scatter.2.cloned.1.call-done = bf16[384,384]{1,0:T(8,128)(2,1)} async-done(((bf16[6144,384]{1,0:T(8,128)(2,1)}), bf16[384,384]{1,0:T(8,128)(2,1)}) %reduce-scatter.2.cloned.1.call-update) | async-done | bytes 294928 | tf_op jit(solution)/shard_map/reduce_scatter | solution.py:82
  (3 shorter events, 0.0 us)
Async XLA Ops:
  7.2 216.7 %copy-start = (bf16[512,384]{1,0:T(8,128)(2,1)S(1)}, bf16[512,384]{1,0:T(8,128)(2,1)}, u32[]{:S(2)}) copy-start(bf16[512,384]{1,0:T(8,128)(2,1)} %param.10) | copy-start | bytes 1179652
  7.2 53.0 %all-gather.5.cloned.1.call-start = ((), (), s32[]{:S(2)}) async-start(), calls=%async_computation.1 | async-start | bytes 6684672 | tf_op jit(solution)/shard_map/all_gather | solution.py:74
  7.9 98.7 %all-gather.7.cloned.1.call-start = ((), (), s32[]{:S(2)}) async-start(), calls=%async_computation.2 | async-start | bytes 6684672 | tf_op jit(solution)/shard_map/all_gather | solution.py:75
  8.7 215.2 %all-gather.9.cloned.1.call-start = ((), (), s32[]{:S(2)}) async-start(), calls=%async_computation.3 | async-start | bytes 6684672 | tf_op jit(solution)/shard_map/all_gather | solution.py:78
  106.7 2.8 copy-start.1
  109.4 2.8 copy-start.2
  112.2 1.0 copy-start.3
  138.4 107.9 %all-gather.11.cloned.1.call-start = ((), (), s32[]{:S(2)}) async-start(), calls=%async_computation.4 | async-start | bytes 7077888 | tf_op jit(solution)/shard_map/all_gather | solution.py:76
  139.0 185.5 %reduce-scatter.2.cloned.1.call-start = ((), (), s32[]{:S(2)}) async-start(), calls=%async_computation.5 | async-start | bytes 5013504 | tf_op jit(solution)/shard_map/reduce_scatter | solution.py:82
Sparse Core Ops, SparseCore 0:
  9.8 50.2 all-gather.4
  62.0 44.6 all-gather.6
  138.6 85.2 all-gather.8
  225.5 20.8 all-gather.10
  249.3 75.2 reduce-scatter.1

commit v2 on v1

--- a/solution.py
+++ b/solution.py
@@ -10,6 +10,12 @@
 
 HD = 128
 BLOCK = 512
+SIDE = 4
+ROWS = SIDE * SIDE
+DEPTH = 8
+HALF = HD // 2
+QUARTER = HD // 4
+MESH = pl.DeviceIdType.MESH
 
 
 def attend_kernel(place_ref, mask_ref, q_ref, k_ref, v_ref, out_ref, run_max, run_sum, weighted):
@@ -39,7 +45,7 @@
 
     @pl.when(back == pl.num_programs(1) - 1)
     def _():
-        out_ref[...] = (weighted[...] / run_sum[...]).astype(out_ref.dtype)
+        out_ref[0] = (weighted[...] / run_sum[...]).T.astype(out_ref.dtype)
 
 
 def attend(place, mask_row, queries, keys, values):
@@ -50,12 +56,12 @@
     q_spec = pl.BlockSpec((BLOCK, HD), lambda h, b, place, mask: (0, h))
     return pl.pallas_call(
         attend_kernel,
-        out_shape=jax.ShapeDtypeStruct((rows, width), jnp.bfloat16),
+        out_shape=jax.ShapeDtypeStruct((heads, HD, rows), jnp.bfloat16),
         grid_spec=pltpu.PrefetchScalarGridSpec(
             num_scalar_prefetch=2,
             grid=(heads, blocks),
             in_specs=[q_spec, kv_spec, kv_spec],
-            out_specs=q_spec,
+            out_specs=pl.BlockSpec((1, HD, BLOCK), lambda h, b, place, mask: (h, 0, 0)),
             scratch_shapes=[
                 pltpu.VMEM((rows, 1), jnp.float32),
                 pltpu.VMEM((rows, 1), jnp.float32),
@@ -68,20 +74,251 @@
     )(place, mask_row, queries, keys, values)
 
 
+def project_kernel(
+    att_ref, w_ref, cot_ref, mixed_ref, grad_ref,
+    gath, weight, mixed_sum, kept, pair_out, pair_in, ring_out, ring_in,
+    ag_send, ag_recv, w_send, w_recv, w_local, pair_send, pair_recv, ring_send, ring_recv,
+):
+    me = lax.axis_index("row")
+    core = lax.axis_index("col")
+    z = lax.axis_index("ctx")
+    here = (lax.rem(me, SIDE), lax.div(me, SIDE))
+    heads = att_ref.shape[0]
+
+    def shifted(value, by, size):
+        return lax.rem(value + (by + size), size)
+
+    def block_at(half, first, second):
+        by = (first, second) if half == 0 else (second, first)
+        return shifted(here[1], by[1], SIDE) * SIDE + shifted(here[0], by[0], SIDE)
+
+    def up(by):
+        return {"ctx": shifted(z, by, DEPTH)}
+
+    sibling = {"col": 1 - core}
+
+    barrier = pltpu.get_barrier_semaphore()
+    for first, second in ((1, 0), (-1, 0), (0, 1), (0, -1)):
+        pl.semaphore_signal(barrier, inc=1, device_id={"row": block_at(0, first, second)}, device_id_type=MESH)
+    for by in (1, -1):
+        pl.semaphore_signal(barrier, inc=1, device_id=up(by), device_id_type=MESH)
+    pl.semaphore_signal(barrier, inc=1, device_id=sibling, device_id_type=MESH)
+    pl.semaphore_wait(barrier, 7)
+
+    def put(e, half, block, quarter, leg, by, slot):
+        low = half * HALF + (0 if quarter is None else quarter * QUARTER)
+        ref = gath.at[e, block, pl.ds(low, HALF if quarter is None else QUARTER)]
+        to = block_at(half, by, 0) if leg == 0 else block_at(half, 0, by)
+        return pltpu.make_async_remote_copy(
+            src_ref=ref, dst_ref=ref, send_sem=ag_send.at[e, half, slot], recv_sem=ag_recv.at[e, half, block],
+            device_id={"row": to}, device_id_type=MESH,
+        )
+
+    def arrived(e, half, block):
+        put(e, half, block, None, 0, 1, 0).wait_recv()
+
+    def send_weight():
+        return pltpu.make_async_remote_copy(
+            src_ref=w_ref, dst_ref=weight.at[core], send_sem=w_send, recv_sem=w_recv,
+            device_id=sibling, device_id_type=MESH,
+        )
+
+    def send_pair(e):
+        return pltpu.make_async_remote_copy(
+            src_ref=pair_out.at[e], dst_ref=pair_in.at[e], send_sem=pair_send.at[e], recv_sem=pair_recv.at[e],
+            device_id=sibling, device_id_type=MESH,
+        )
+
+    def send_ring(e, way, step):
+        rows = pl.ds(way * HALF, HALF) if step == 0 else pl.ds(0, HD)
+        return pltpu.make_async_remote_copy(
+            src_ref=ring_out.at[e, way, step, rows], dst_ref=ring_in.at[e, way, step, rows],
+            send_sem=ring_send.at[e, way, step], recv_sem=ring_recv.at[e, way, step],
+            device_id=up(1 - 2 * way), device_id_type=MESH,
+        )
+
+    @pl.loop(0, heads)
+    def _(e):
+        gath[e, me] = att_ref[e]
+        for half in (0, 1):
+            for slot, (leg, by) in enumerate(((0, 1), (0, -1), (1, 1), (1, -1))):
+                put(e, half, me, None, leg, by, slot).start()
+
+    send_weight().start()
+    own_weight = pltpu.make_async_copy(w_ref, weight.at[core], w_local)
+    own_weight.start()
+    mixed_sum[...] = jnp.zeros_like(mixed_sum)
+    own_weight.wait()
+
+    def gather_first(e):
+        for half in (0, 1):
+            for by in (-1, 1):
+                block = block_at(half, by, 0)
+                arrived(e, half, block)
+                base = 4 if by == -1 else 6
+                put(e, half, block, 0 if by == -1 else 1, 0, -by, 10 if by == -1 else 11).start()
+                put(e, half, block, None, 1, 1, base).start()
+                put(e, half, block, None, 1, -1, base + 1).start()
+
+    def gather_opposite(e):
+        for half in (0, 1):
+            block = block_at(half, 2, 0)
+            arrived(e, half, block)
+            put(e, half, block, None, 1, 1, 8).start()
+            put(e, half, block, None, 1, -1, 9).start()
+
+    def gather_line(e, first, at):
+        for half in (0, 1):
+            for by in (-1, 1):
+                block = block_at(half, first, by)
+                arrived(e, half, block)
+                put(e, half, block, 0 if by == -1 else 1, 1, -by, 12 + 2 * at + (0 if by == -1 else 1)).start()
+
+    def gather_rest(e):
+        for half in (0, 1):
+            for first in (0, -1, 1, 2):
+                arrived(e, half, block_at(half, first, 2))
+
+    def gradient_parts(e):
+        for part in (0, 1):
+            for_sibling = gath[e, pl.ds((1 - core) * DEPTH + part * 4, 4)].reshape(4 * HD, BLOCK)
+            pair_out[e, pl.ds(part * 4, 4)] = (
+                jnp.dot(for_sibling, cot_ref[...], preferred_element_type=jnp.float32)
+                .astype(jnp.bfloat16).reshape(4, HD, cot_ref.shape[1])
+            )
+        send_pair(e).start()
+        for part in (0, 1):
+            for_me = gath[e, pl.ds(core * DEPTH + part * 4, 4)].reshape(4 * HD, BLOCK)
+            kept[e, pl.ds(part * 4, 4)] = jnp.dot(
+                for_me, cot_ref[...], preferred_element_type=jnp.float32
+            ).reshape(4, HD, cot_ref.shape[1])
+
+    def mix(e):
+        @pl.loop(0, ROWS // 4)
+        def _(part):
+            blocks = gath[e, pl.ds(part * 4, 4)].reshape(4 * HD, BLOCK)
+            matrix = weight[lax.div(part, 2), pl.ds(lax.rem(part, 2) * 4, 4), e].reshape(4 * HD, cot_ref.shape[1])
+            mixed_sum[...] += lax.dot_general(
+                blocks, matrix, (((0,), (0,)), ((), ())), preferred_element_type=jnp.float32
+            )
+
+    def chip_part(e, target):
+        return kept[e, target] + pair_in[e, target].astype(jnp.float32)
+
+    def ring_start(e):
+        send_pair(e).wait_recv()
+        for way in (0, 1):
+            target = shifted(z, 4, DEPTH)
+            rows = pl.ds(way * HALF, HALF)
+            ring_out[e, way, 0, rows] = (
+                kept[e, target, rows] + pair_in[e, target, rows].astype(jnp.float32)
+            ).astype(jnp.bfloat16)
+            send_ring(e, way, 0).start()
+
+    def ring_step(e, step):
+        for way in (0, 1):
+            send_ring(e, way, step - 1).wait_recv()
+            target = shifted(z, (4 - step) * (1 - 2 * way), DEPTH)
+            for half in (0, 1):
+                rows = pl.ds(half * HALF, HALF)
+                total = kept[e, target, rows] + pair_in[e, target, rows].astype(jnp.float32)
+                if step > 1 or half == way:
+                    total += ring_in[e, way, step - 1, rows].astype(jnp.float32)
+                ring_out[e, way, step, rows] = total.astype(jnp.bfloat16)
+            send_ring(e, way, step).start()
+
+    def ring_end(e):
+        send_ring(e, 0, 3).wait_recv()
+        send_ring(e, 1, 3).wait_recv()
+        total = chip_part(e, z) + ring_in[e, 0, 3].astype(jnp.float32) + ring_in[e, 1, 3].astype(jnp.float32)
+        grad_ref[e] = total.astype(jnp.bfloat16)
+
+    @pl.loop(0, heads + 1)
+    def _(it):
+        gathers = it < heads
+        reduces = it > 0
+        e = jnp.minimum(it, heads - 1)
+        b = jnp.maximum(it - 1, 0)
+        pl.when(reduces)(lambda: gradient_parts(b))
+        pl.when(gathers)(lambda: gather_first(e))
+        pl.when(reduces)(lambda: ring_start(b))
+        pl.when(gathers)(lambda: gather_opposite(e))
+        pl.when(it == 1)(lambda: send_weight().wait_recv())
+        pl.when(reduces)(lambda: mix(b))
+        pl.when(gathers)(lambda: gather_line(e, 0, 0))
+        pl.when(reduces)(lambda: ring_step(b, 1))
+        pl.when(gathers)(lambda: gather_line(e, -1, 1))
+        pl.when(reduces)(lambda: ring_step(b, 2))
+        pl.when(gathers)(lambda: gather_line(e, 1, 2))
+        pl.when(reduces)(lambda: ring_step(b, 3))
+        pl.when(gathers)(lambda: gather_line(e, 2, 3))
+        pl.when(gathers)(lambda: gather_rest(e))
+        pl.when(reduces)(lambda: ring_end(b))
+
+    mixed_ref[...] = mixed_sum[...].astype(jnp.bfloat16)
+
+    send_weight().wait_send()
+
+    @pl.loop(0, heads)
+    def _(e):
+        for half in (0, 1):
+            @pl.loop(0, 10)
+            def _(slot):
+                put(e, half, me, None, 0, 1, slot).wait_send()
+
+            @pl.loop(10, 20)
+            def _(slot):
+                put(e, half, me, 0, 0, 1, slot).wait_send()
+
+        send_pair(e).wait_send()
+        for way in (0, 1):
+            for step in range(4):
+                send_ring(e, way, step).wait_send()
+
+
+def project(attended, weight_half, cotangent):
+    heads = attended.shape[0]
+    width = cotangent.shape[1]
+    vmem = pl.BlockSpec(memory_space=pltpu.VMEM)
+    dma = pltpu.SemaphoreType.DMA
+    low = jnp.bfloat16
+    return pl.pallas_call(
+        project_kernel,
+        out_shape=(
+            jax.ShapeDtypeStruct((BLOCK, width), low),
+            jax.ShapeDtypeStruct((heads, HD, width), low),
+        ),
+        in_specs=[vmem] * 3,
+        out_specs=(vmem, vmem),
+        scratch_shapes=[
+            pltpu.VMEM((heads, ROWS, HD, BLOCK), low),
+            pltpu.VMEM((2, ROWS // 2, heads, HD, width), low),
+            pltpu.VMEM((BLOCK, width), jnp.float32),
+            pltpu.VMEM((heads, DEPTH, HD, width), jnp.float32),
+            pltpu.VMEM((heads, DEPTH, HD, width), low),
+            pltpu.VMEM((heads, DEPTH, HD, width), low),
+            pltpu.VMEM((heads, 2, 4, HD, width), low),
+            pltpu.VMEM((heads, 2, 4, HD, width), low),
+            dma((heads, 2, 20)), dma((heads, 2, ROWS)), dma, dma, dma,
+            dma((heads,)), dma((heads,)), dma((heads, 2, 4)), dma((heads, 2, 4)),
+        ],
+        compiler_params=pltpu.CompilerParams(
+            collective_id=1, has_side_effects=True, vmem_limit_bytes=56 << 20
+        ),
+    )(attended, weight_half, cotangent)
+
+
 def body(queries, keys, values, out_weight, cotangent, block_mask):
     place = lax.axis_index(("col", "ctx"))
+    width = queries.shape[1]
     mask_row = lax.dynamic_index_in_dim(block_mask, place, 0, keepdims=False)
     all_keys = lax.all_gather(keys, ("col", "ctx"), axis=0, tiled=True)
     all_values = lax.all_gather(values, ("col", "ctx"), axis=0, tiled=True)
-    weight = lax.all_gather(out_weight, "col", axis=0, tiled=True)
     attended = attend(place.reshape(1), mask_row, queries, all_keys, all_values)
-    all_heads = lax.all_gather(attended, "row", axis=1, tiled=True)
-    partial = lax.dot_general(
-        all_heads, cotangent, (((0,), (0,)), ((), ())), preferred_element_type=jnp.float32
-    ).astype(jnp.bfloat16)
-    grad_weight = lax.psum_scatter(partial, ("col", "ctx"), scatter_dimension=0, tiled=True)
-    mixed_out = jnp.dot(all_heads, weight, preferred_element_type=jnp.float32)
-    return (mixed_out.astype(jnp.bfloat16), grad_weight)
+    mixed_out, grad_weight = project(
+        attended, out_weight.reshape(ROWS // 2, width // HD, HD, width), cotangent
+    )
+    return (mixed_out, grad_weight.reshape(width, width))
 
 
 def solution(mesh):

time: 331 us -> 258 us (0.78)
  waiting for transfers between devices: 268 us -> 99.3 us
  Pallas kernels: 25.2 us -> 133 us
  matrix products: 16.8 us -> 0 us
  local copies, waits for them, and re-layouts: 7.27 us -> 10.8 us
    pallas_call x1 -> x2, Pallas kernels: 25.2 us -> 133 us  [the longest x1 109 us: project(): pl.pallas_call(project_kernel, out_shape=(jax.ShapeDtypeStruct((BLOCK, wi...]
    all_gather x2 -> x0, waiting for transfers between devices: 98.8 us -> none  [the longest x1 84.7 us: body(): all_heads = lax.all_gather(attended, 'row', axis=1, tiled=True)]
    reduce_scatter x1 -> x0, waiting for transfers between devices: 69.9 us -> none  [body(): lax.psum_scatter(partial, ('col', 'ctx'), scatter_dimension=0, tiled=True)]
    dot_general x2 -> x0, matrix products: 16.8 us -> none  [the longest x1 8.46 us: body(): lax.dot_general(all_heads, cotangent, (((0,), (0,)), ((), ())), preferred...]
    unnamed x8 -> x12, local copies, waits for them, and re-layouts: 6.57 us -> 10.8 us
  transfers between devices with their start and end apart: 5 -> 2, of which waited for: 5 -> 2; matrix products, arithmetic and copies ran while one was open for 5% -> 0% of each run, Pallas kernels for 0% -> 0%
where the time goes in v2:
time: 258 us
  Pallas kernels  133 us (52%)
  waiting for transfers between devices  99.3 us (38%)
  between operations  14.1 us (5%)
  local copies, waits for them, and re-layouts  10.8 us (4%)
    pallas_call x1, Pallas kernels, project(): pl.pallas_call(project_kernel, out_shape=(jax.ShapeDtypeStruct((BLOCK, wi...  109 us
    all_gather x1, waiting for transfers between devices, body(): all_keys = lax.all_gather(keys, ('col', 'ctx'), axis=0, tiled=True)  51.4 us
    all_gather x1, waiting for transfers between devices, body(): all_values = lax.all_gather(values, ('col', 'ctx'), axis=0, tiled=True)  46.5 us
    pallas_call x1, Pallas kernels, attend(): pl.pallas_call(attend_kernel, out_shape=jax.ShapeDtypeStruct((heads, HD,...  24.5 us
    unnamed x12, local copies, waits for them, and re-layouts  10.8 us
  transfers between devices with their start and end apart: 2, of which 2 were waited for; matrix products, arithmetic and copies ran while one was open for 0% of the time, Pallas kernels for 0%

profile of v2, /device:TPU:1, one launch (start us, length us, event | category | flops | bytes accessed | tf_op | source)
XLA Modules:
  0.0 257.7 jit_solution(8987817350627434637)
XLA Ops:
  7.2 0.0 copy-start
  7.2 0.0 all-gather.3.cloned.1.call-start
  7.2 0.7 all-gather.3.cloned.1.call-update
  7.9 0.0 all-gather.5.cloned.1.call-start
  8.0 0.7 all-gather.5.cloned.1.call-update
  8.7 0.0 copy-done
  8.7 51.4 %all-gather.3.cloned.1.call-done.k_ref = bf16[8192,384]{1,0:T(8,128)(2,1)} async-done(((bf16[512,384]{1,0:T(8,128)(2,1)}), bf16[8192,384]{1,0:T(8,128)(2,1)}) %all-gather.3.cloned.1.call-update) | async-done | bytes 6291472 | tf_op jit(solution)/shard_map/all_gather | solution.py:315
  60.1 46.5 %all-gather.5.cloned.1.call-done.v_ref = bf16[8192,384]{1,0:T(8,128)(2,1)} async-done(((bf16[512,384]{1,0:T(8,128)(2,1)}), bf16[8192,384]{1,0:T(8,128)(2,1)}) %all-gather.5.cloned.1.call-update) | async-done | bytes 6291472 | tf_op jit(solution)/shard_map/all_gather | solution.py:316
  106.7 0.0 copy-start.1
  106.7 2.8 %copy-done.1 = bf16[8192,384]{1,0:T(8,128)(2,1)S(1)} copy-done((bf16[8192,384]{1,0:T(8,128)(2,1)S(1)}, bf16[8192,384]{1,0:T(8,128)(2,1)}, u32[]{:S(2)}) %copy-start.1) | copy-done | bytes 6291480
  109.4 0.0 copy-start.2
  109.4 2.8 %copy-done.2 = bf16[8192,384]{1,0:T(8,128)(2,1)S(1)} copy-done((bf16[8192,384]{1,0:T(8,128)(2,1)S(1)}, bf16[8192,384]{1,0:T(8,128)(2,1)}, u32[]{:S(2)}) %copy-start.2) | copy-done | bytes 6291480
  112.2 0.0 copy-start.4
  112.2 1.0 copy-done.4
  113.2 24.5 %shard_map.77.att_ref = bf16[3,128,512]{2,1,0:T(8,128)(2,1)S(1)} custom-call(s32[1]{0:T(128)} %bitcast.place_ref, s32[16]{0:T(128)S(1)} %dynamic-slice_bitcast_fusion.mask_ref, bf16[512,384]{1,0:T(8,128)(2,1)S(1)} %copy-done.4, bf16[8192,384]{1,0:T(8,128)(2,1)S(1)} %copy-done.1, bf16[8192,384]{1,0:T(8,128)(2,1)S(1)} %copy-done.2), custom_call_target="tpu_custom_call" | custom-call | tf_op jit(solution)/shard_map/pallas_call | solution.py:57
  137.7 0.0 copy-start.3
  137.8 0.7 copy-done.3
  138.5 108.9 %shard_map.78 = (bf16[512,384]{1,0:T(8,128)(2,1)}, bf16[3,128,384]{2,1,0:T(8,128)(2,1)}) custom-call(bf16[3,128,512]{2,1,0:T(8,128)(2,1)} %copy-done.3, bf16[8,3,128,384]{3,2,1,0:T(8,128)(2,1)} %bitcast.5, bf16[512,384]{1,0:T(8,128)(2,1)} %cot_ref.1), custom_call_target="tpu_custom_call" | custom-call | tf_op jit(solution)/shard_map/pallas_call | solution.py:285
  247.4 1.8 copy.10
  249.2 1.7 copy.11
  (1 shorter events, 0.0 us)
Async XLA Ops:
  7.2 1.5 copy-start
  7.2 53.0 %all-gather.3.cloned.1.call-start = ((), (), s32[]{:S(2)}) async-start(), calls=%async_computation | async-start | bytes 6684672 | tf_op jit(solution)/shard_map/all_gather | solution.py:315
  7.9 98.7 %all-gather.5.cloned.1.call-start = ((), (), s32[]{:S(2)}) async-start(), calls=%async_computation.1 | async-start | bytes 6684672 | tf_op jit(solution)/shard_map/all_gather | solution.py:316
  106.7 2.8 %copy-start.1 = (bf16[8192,384]{1,0:T(8,128)(2,1)S(1)}, bf16[8192,384]{1,0:T(8,128)(2,1)}, u32[]{:S(2)}) copy-start(bf16[8192,384]{1,0:T(8,128)(2,1)} %all-gather.3.cloned.1.call-done.k_ref) | copy-start | bytes 18874372
  109.4 2.8 %copy-start.2 = (bf16[8192,384]{1,0:T(8,128)(2,1)S(1)}, bf16[8192,384]{1,0:T(8,128)(2,1)}, u32[]{:S(2)}) copy-start(bf16[8192,384]{1,0:T(8,128)(2,1)} %all-gather.5.cloned.1.call-done.v_ref) | copy-start | bytes 18874372
  112.2 1.0 copy-start.4
  137.7 0.7 copy-start.3
Sparse Core Ops, SparseCore 0:
  9.8 50.2 all-gather.2
  62.0 44.6 all-gather.4

commit v3 on v2

--- a/solution.py
+++ b/solution.py
@@ -18,60 +18,161 @@
 MESH = pl.DeviceIdType.MESH
 
 
-def attend_kernel(place_ref, mask_ref, q_ref, k_ref, v_ref, out_ref, run_max, run_sum, weighted):
-    back = pl.program_id(1)
-    block = place_ref[0] - back
+def shifted(value, by, size):
+    return lax.rem(value + (by + size), size)
+
+
+def attend_kernel(
+    mask_ref, q_ref, k_ref, v_ref, out_ref,
+    queries, keys, values, run_max, run_sum, weighted, ring_send, ring_recv, pair_send, pair_recv,
+):
+    core = lax.axis_index("col")
+    z = lax.axis_index("ctx")
+    heads = out_ref.shape[0]
     rate = math.log2(math.e) / math.sqrt(HD)
-
-    @pl.when(back == 0)
-    def _():
-        run_max[...] = jnp.full_like(run_max, -1e30)
-        run_sum[...] = jnp.zeros_like(run_sum)
-        weighted[...] = jnp.zeros_like(weighted)
-
-    @pl.when((block >= 0) & (mask_ref[jnp.maximum(block, 0)] == 1))
-    def _():
-        scores = lax.dot_general(
-            q_ref[...], k_ref[...], (((1,), (1,)), ((), ())), preferred_element_type=jnp.float32
-        )
-        new_max = jnp.maximum(run_max[...], jnp.max(scores, axis=1, keepdims=True))
-        correction = jnp.exp2((run_max[...] - new_max) * rate)
-        weights = jnp.exp2((scores - new_max) * rate)
-        run_sum[...] = run_sum[...] * correction + jnp.sum(weights, axis=1, keepdims=True)
-        weighted[...] = weighted[...] * correction + jnp.dot(
-            weights.astype(jnp.bfloat16), v_ref[...], preferred_element_type=jnp.float32
-        )
-        run_max[...] = new_max
-
-    @pl.when(back == pl.num_programs(1) - 1)
-    def _():
-        out_ref[0] = (weighted[...] / run_sum[...]).T.astype(out_ref.dtype)
-
-
-def attend(place, mask_row, queries, keys, values):
+    stores = (keys, values)
+    is_key, is_value = 0, 1
+
+    barrier = pltpu.get_barrier_semaphore()
+    for by in (1, -1):
+        pl.semaphore_signal(barrier, inc=1, device_id={"ctx": shifted(z, by, DEPTH)}, device_id_type=MESH)
+    pl.semaphore_signal(barrier, inc=1, device_id={"col": 1 - core}, device_id_type=MESH)
+    for e in range(heads):
+        columns = slice(e * HD, (e + 1) * HD)
+        keys[core, z, e] = k_ref[:, columns]
+    pl.semaphore_wait(barrier, 3)
+
+    def ring(kind, e, block, by):
+        ref = stores[kind].at[core, block, e]
+        way = 0 if by == 1 else 1
+        return pltpu.make_async_remote_copy(
+            src_ref=ref, dst_ref=ref, send_sem=ring_send.at[way, kind, block, e], recv_sem=ring_recv.at[kind, block, e],
+            device_id={"ctx": shifted(z, by, DEPTH)}, device_id_type=MESH,
+        )
+
+    def pair(kind, e, block):
+        ref = stores[kind].at[0, block, e]
+        return pltpu.make_async_remote_copy(
+            src_ref=ref, dst_ref=ref, send_sem=pair_send.at[kind, block, e], recv_sem=pair_recv.at[kind, block, e],
+            device_id={"col": 1 - core}, device_id_type=MESH,
+        )
+
+    def hand_over(kind, e, block):
+        pl.when(core == 0)(lambda: pair(kind, e, block).start())
+
+    for kind in (is_key, is_value):
+        for e in range(heads):
+            if kind == is_value:
+                values[core, z, e] = v_ref[:, e * HD:(e + 1) * HD].T
+            ring(kind, e, z, 1).start()
+            ring(kind, e, z, -1).start()
+            hand_over(kind, e, z)
+
+    for e in range(heads):
+        queries[e] = q_ref[:, e * HD:(e + 1) * HD]
+    run_max[...] = jnp.full_like(run_max, -1e30)
+    run_sum[...] = jnp.zeros_like(run_sum)
+    weighted[...] = jnp.zeros_like(weighted)
+
+    def pass_on(hop):
+        @pl.loop(0, heads)
+        def _(e):
+            for kind in (is_key, is_value):
+                for by in (1, -1):
+                    longer = (kind == is_key) == (by == 1)
+                    if hop == 4 and not longer:
+                        continue
+                    block = shifted(z, -by * hop, DEPTH)
+                    ring(kind, e, block, by).wait_recv()
+                    if hop < 3 or (hop == 3 and longer):
+                        ring(kind, e, block, by).start()
+                    hand_over(kind, e, block)
+
+    def absorb(e, group, blocks):
+        row = core * DEPTH + z
+        query = queries[e]
+        parts = []
+        new_max = run_max[e]
+        for block in blocks:
+            penalty = jnp.where(mask_ref[row, group * DEPTH + block] == 1, 0.0, 1e30)
+            scores = lax.dot_general(
+                keys[group, block, e], query, (((1,), (1,)), ((), ())), preferred_element_type=jnp.float32
+            )
+            new_max = jnp.maximum(new_max, jnp.max(scores, axis=0, keepdims=True) - penalty)
+            parts.append((block, penalty, scores))
+        correction = jnp.exp2((run_max[e] - new_max) * rate)
+        total = run_sum[e] * correction
+        product = weighted[e] * correction
+        for block, penalty, scores in parts:
+            probs = jnp.exp2(scores * rate - (new_max * rate + penalty))
+            total += jnp.sum(probs, axis=0, keepdims=True)
+            product += jnp.dot(
+                values[group, block, e], probs.astype(jnp.bfloat16), preferred_element_type=jnp.float32
+            )
+        run_max[e] = new_max
+        run_sum[e] = total
+        weighted[e] = product
+
+    def compute(hop):
+        blocks = [shifted(z, by * hop, DEPTH) for by in ((1, -1) if 0 < hop < 4 else (1,))]
+
+        @pl.loop(0, heads)
+        def _(e):
+            absorb(e, core, blocks)
+
+            @pl.when(core == 1)
+            def _():
+                for block in blocks:
+                    for kind in (is_key, is_value):
+                        pair(kind, e, block).wait_recv()
+                absorb(e, 0, blocks)
+
+    for hop in range(1, 5):
+        pass_on(hop)
+        compute(hop - 1)
+    compute(4)
+
+    @pl.loop(0, heads)
+    def _(e):
+        out_ref[e] = (weighted[e] / run_sum[e]).astype(out_ref.dtype)
+
+    @pl.loop(0, heads)
+    def _(e):
+        for kind in (is_key, is_value):
+            for by in (1, -1):
+                for hop in range(4 if (kind == is_key) == (by == 1) else 3):
+                    ring(kind, e, shifted(z, -by * hop, DEPTH), by).wait_send()
+
+            @pl.when(core == 0)
+            def _():
+                @pl.loop(0, DEPTH)
+                def _(block):
+                    pair(kind, e, block).wait_send()
+
+
+def attend(block_mask, queries, keys, values):
     rows, width = queries.shape
-    blocks = keys.shape[0] // BLOCK
     heads = width // HD
-    kv_spec = pl.BlockSpec((BLOCK, HD), lambda h, b, place, mask: (jnp.maximum(place[0] - b, 0), h))
-    q_spec = pl.BlockSpec((BLOCK, HD), lambda h, b, place, mask: (0, h))
+    vmem = pl.BlockSpec(memory_space=pltpu.VMEM)
+    dma = pltpu.SemaphoreType.DMA
     return pl.pallas_call(
         attend_kernel,
         out_shape=jax.ShapeDtypeStruct((heads, HD, rows), jnp.bfloat16),
-        grid_spec=pltpu.PrefetchScalarGridSpec(
-            num_scalar_prefetch=2,
-            grid=(heads, blocks),
-            in_specs=[q_spec, kv_spec, kv_spec],
-            out_specs=pl.BlockSpec((1, HD, BLOCK), lambda h, b, place, mask: (h, 0, 0)),
-            scratch_shapes=[
-                pltpu.VMEM((rows, 1), jnp.float32),
-                pltpu.VMEM((rows, 1), jnp.float32),
-                pltpu.VMEM((rows, HD), jnp.float32),
-            ],
+        in_specs=[pl.BlockSpec(memory_space=pltpu.SMEM), vmem, vmem, vmem],
+        out_specs=vmem,
+        scratch_shapes=[
+            pltpu.VMEM((heads, BLOCK, HD), jnp.bfloat16),
+            pltpu.VMEM((2, DEPTH, heads, BLOCK, HD), jnp.bfloat16),
+            pltpu.VMEM((2, DEPTH, heads, HD, BLOCK), jnp.bfloat16),
+            pltpu.VMEM((heads, 1, BLOCK), jnp.float32),
+            pltpu.VMEM((heads, 1, BLOCK), jnp.float32),
+            pltpu.VMEM((heads, HD, BLOCK), jnp.float32),
+            dma((2, 2, DEPTH, heads)), dma((2, DEPTH, heads)), dma((2, DEPTH, heads)), dma((2, DEPTH, heads)),
+        ],
+        compiler_params=pltpu.CompilerParams(
+            collective_id=0, has_side_effects=True, vmem_limit_bytes=56 << 20
         ),
-        compiler_params=pltpu.CompilerParams(
-            dimension_semantics=("arbitrary", "arbitrary"), vmem_limit_bytes=32 << 20
-        ),
-    )(place, mask_row, queries, keys, values)
+    )(block_mask, queries, keys, values)
 
 
 def project_kernel(
@@ -84,9 +185,6 @@
     z = lax.axis_index("ctx")
     here = (lax.rem(me, SIDE), lax.div(me, SIDE))
     heads = att_ref.shape[0]
-
-    def shifted(value, by, size):
-        return lax.rem(value + (by + size), size)
 
     def block_at(half, first, second):
         by = (first, second) if half == 0 else (second, first)
@@ -309,12 +407,8 @@
 
 
 def body(queries, keys, values, out_weight, cotangent, block_mask):
-    place = lax.axis_index(("col", "ctx"))
     width = queries.shape[1]
-    mask_row = lax.dynamic_index_in_dim(block_mask, place, 0, keepdims=False)
-    all_keys = lax.all_gather(keys, ("col", "ctx"), axis=0, tiled=True)
-    all_values = lax.all_gather(values, ("col", "ctx"), axis=0, tiled=True)
-    attended = attend(place.reshape(1), mask_row, queries, all_keys, all_values)
+    attended = attend(block_mask, queries, keys, values)
     mixed_out, grad_weight = project(
         attended, out_weight.reshape(ROWS // 2, width // HD, HD, width), cotangent
     )

time: 258 us -> 179 us (0.69)
  waiting for transfers between devices: 99.3 us -> 0 us
  Pallas kernels: 133 us -> 175 us
  between operations: 14.1 us -> 0.65 us
  local copies, waits for them, and re-layouts: 10.8 us -> 3.49 us
    all_gather x2 -> x0, waiting for transfers between devices: 98 us -> none  [the longest x1 51.4 us: body(): all_keys = lax.all_gather(keys, ('col', 'ctx'), axis=0, tiled=True)]
    pallas_call x1, Pallas kernels: 24.5 us -> 82.1 us  [attend(): pl.pallas_call(attend_kernel, out_shape=jax.ShapeDtypeStruct((heads, HD,...]
    pallas_call x1, Pallas kernels: 109 us -> 92.9 us  [project(): pl.pallas_call(project_kernel, out_shape=(jax.ShapeDtypeStruct((BLOCK, wi...]
    unnamed x12 -> x2, local copies, waits for them, and re-layouts: 10.8 us -> 3.49 us
  transfers between devices with their start and end apart: 2 -> 0, of which waited for: 2 -> 0; matrix products, arithmetic and copies ran while one was open for 0% -> 0% of each run, Pallas kernels for 0% -> 0%
where the time goes in v3:
time: 179 us
  Pallas kernels  175 us (98%)
  local copies, waits for them, and re-layouts  3.49 us (2%)
    pallas_call x1, Pallas kernels, project(): pl.pallas_call(project_kernel, out_shape=(jax.ShapeDtypeStruct((BLOCK, wi...  92.9 us
    pallas_call x1, Pallas kernels, attend(): pl.pallas_call(attend_kernel, out_shape=jax.ShapeDtypeStruct((heads, HD,...  82.1 us

profile of v3, /device:TPU:1, one launch (start us, length us, event | category | flops | bytes accessed | tf_op | source)
XLA Modules:
  0.0 179.2 jit_solution(11408483849927403396)
XLA Ops:
  0.6 82.1 %shard_map.77.att_ref = bf16[3,128,512]{2,1,0:T(8,128)(2,1)} custom-call(s32[16,16]{1,0:T(8,128)} %mask_ref.1, bf16[512,384]{1,0:T(8,128)(2,1)} %q_ref.1, bf16[512,384]{1,0:T(8,128)(2,1)} %k_ref.1, bf16[512,384]{1,0:T(8,128)(2,1)} %v_ref.1), custom_call_target="tpu_custom_call" | custom-call | tf_op jit(solution)/shard_map/pallas_call | solution.py:158
  82.8 92.9 %shard_map.78 = (bf16[512,384]{1,0:T(8,128)(2,1)}, bf16[3,128,384]{2,1,0:T(8,128)(2,1)}) custom-call(bf16[3,128,512]{2,1,0:T(8,128)(2,1)} %shard_map.77.att_ref, bf16[8,3,128,384]{3,2,1,0:T(8,128)(2,1)} %bitcast.2, bf16[512,384]{1,0:T(8,128)(2,1)} %cot_ref.1), custom_call_target="tpu_custom_call" | custom-call | tf_op jit(solution)/shard_map/pallas_call | solution.py:383
  175.7 1.8 copy.10
  177.5 1.7 copy.11

commit v4 on v2

v4 whole, which is shorter than its diff:
```python
import functools
import math

import jax
import jax.numpy as jnp
from jax import lax
from jax.experimental import pallas as pl
from jax.experimental.pallas import tpu as pltpu
from jax.sharding import PartitionSpec as P

HD = 128
BLOCK = 512
SIDE = 4
ROWS = SIDE * SIDE
DEPTH = 8
HALF = HD // 2
QUARTER = HD // 4
MESH = pl.DeviceIdType.MESH


def shifted(value, by, size):
    return lax.rem(value + (by + size), size)


def layer_kernel(
    mask_ref, q_ref, k_ref, v_ref, w_ref, cot_ref, mixed_ref, grad_ref,
    queries, keys, values, run_max, run_sum, weighted,
    gath, weight, cot, mixed_sum, kept, pair_out, pair_in, ring_out, ring_in,
    kv_send, kv_recv, hand_send, hand_recv, ag_send, ag_recv,
    w_send, w_recv, local, pair_send, pair_recv, ring_send, ring_recv,
):
    me = lax.axis_index("row")
    core = lax.axis_index("col")
    z = lax.axis_index("ctx")
    here = (lax.rem(me, SIDE), lax.div(me, SIDE))
    heads = grad_ref.shape[0]
    width = cot_ref.shape[1]
    rate = math.log2(math.e) / math.sqrt(HD)
    stores = (keys, values)
    is_key, is_value = 0, 1
    sibling = {"col": 1 - core}

    def up(by):
        return {"ctx": shifted(z, by, DEPTH)}

    def block_at(half, first, second):
        by = (first, second) if half == 0 else (second, first)
        return shifted(here[1], by[1], SIDE) * SIDE + shifted(here[0], by[0], SIDE)

    fetch_weight = pltpu.make_async_copy(w_ref, weight.at[core], local.at[0])
    fetch_cot = pltpu.make_async_copy(cot_ref, cot, local.at[1])

    barrier = pltpu.get_barrier_semaphore()
    for first, second in ((1, 0), (-1, 0), (2, 0), (0, 1), (0, -1), (0, 2)):
        pl.semaphore_signal(barrier, inc=1, device_id={"row": block_at(0, first, second)}, device_id_type=MESH)
    for by in (1, -1):
        pl.semaphore_signal(barrier, inc=1, device_id=up(by), device_id_type=MESH)
    pl.semaphore_signal(barrier, inc=1, device_id=sibling, device_id_type=MESH)
    fetch_weight.start()
    fetch_cot.start()
    for e in range(heads):
        keys[core, z, e] = k_ref[:, e * HD:(e + 1) * HD]
    pl.semaphore_wait(barrier, 9)

    def kv(kind, e, block, by):
        ref = stores[kind].at[core, block, e]
        way = 0 if by == 1 else 1
        return pltpu.make_async_remote_copy(
            src_ref=ref, dst_ref=ref, send_sem=kv_send.at[way, kind, block, e], recv_sem=kv_recv.at[kind, block, e],
            device_id=up(by), device_id_type=MESH,
        )

    def hand(kind, e, block):
        ref = stores[kind].at[0, block, e]
        return pltpu.make_async_remote_copy(
            src_ref=ref, dst_ref=ref, send_sem=hand_send.at[kind, block, e], recv_sem=hand_recv.at[kind, block, e],
            device_id=sibling, device_id_type=MESH,
        )

    def hand_over(kind, e, block):
        pl.when(core == 0)(lambda: hand(kind, e, block).start())

    def kv_own(e):
        for kind in (is_key, is_value):
            if kind == is_value:
                values[core, z, e] = v_ref[:, e * HD:(e + 1) * HD].T
            kv(kind, e, z, 1).start()
            kv(kind, e, z, -1).start()
            hand_over(kind, e, z)

    def kv_pass(e, hop):
        for kind in (is_key, is_value):
            for by in (1, -1):
                longer = (kind == is_key) == (by == 1)
                if hop == 4 and not longer:
                    continue
                block = shifted(z, -by * hop, DEPTH)
                kv(kind, e, block, by).wait_recv()
                if hop < 3 or (hop == 3 and longer):
                    kv(kind, e, block, by).start()
                hand_over(kind, e, block)

    def absorb(e, group, blocks):
        row = core * DEPTH + z
        query = queries[e]
        parts = []
        new_max = run_max[e]
        for block in blocks:
            penalty = jnp.where(mask_ref[row, group * DEPTH + block] == 1, 0.0, 1e30)
            scores = lax.dot_general(
                keys[group, block, e], query, (((1,), (1,)), ((), ())), preferred_element_type=jnp.float32
            )
            new_max = jnp.maximum(new_max, jnp.max(scores, axis=0, keepdims=True) - penalty)
            parts.append((block, penalty, scores))
        correction = jnp.exp2((run_max[e] - new_max) * rate)
        total = run_sum[e] * correction
        product = weighted[e] * correction
        for block, penalty, scores in parts:
            probs = jnp.exp2(scores * rate - (new_max * rate + penalty))
            total += jnp.sum(probs, axis=0, keepdims=True)
            product += jnp.dot(
                values[group, block, e], probs.astype(jnp.bfloat16), preferred_element_type=jnp.float32
            )
        run_max[e] = new_max
        run_sum[e] = total
        weighted[e] = product

    def compute(e, hop):
        blocks = [shifted(z, by * hop, DEPTH) for by in ((1, -1) if 0 < hop < 4 else (1,))]

        @pl.loop(0, 1 + core)
        def _(turn):
            @pl.when(turn == 1)
            def _():
                for block in blocks:
                    for kind in (is_key, is_value):
                        hand(kind, e, block).wait_recv()
            absorb(e, core - turn, blocks)

    def put(e, half, block, quarter, leg, by, slot):
        low = half * HALF + (0 if quarter is None else quarter * QUARTER)
        ref = gath.at[e, block, pl.ds(low, HALF if quarter is None else QUARTER)]
        to = block_at(half, by, 0) if leg == 0 else block_at(half, 0, by)
        return pltpu.make_async_remote_copy(
            src_ref=ref, dst_ref=ref, send_sem=ag_send.at[e, half, slot], recv_sem=ag_recv.at[e, half, block],
            device_id={"row": to}, device_id_type=MESH,
        )

    def arrived(e, half, block):
        put(e, half, block, None, 0, 1, 0).wait_recv()

    def gather_own(e):
        gath[e, me] = (weighted[e] / run_sum[e]).astype(gath.dtype)
        for slot, (leg, by) in enumerate(((0, 1), (0, -1), (0, 2), (1, 1), (1, -1))):
            for half in (0, 1):
                put(e, half, me, None, leg, by, slot).start()

    def gather_first(e, by):
        for half in (0, 1):
            block = block_at(half, by, 0)
            arrived(e, half, block)
            base = {-1: 5, 1: 7, 2: 9}[by]
            put(e, half, block, None, 1, 1, base).start()
            put(e, half, block, None, 1, -1, base + 1).start()

    def gather_line(e, first):
        at = {0: 11, -1: 13, 1: 15, 2: 17}[first]
        for half in (0, 1):
            for by in (-1, 1):
                block = block_at(half, first, by)
                arrived(e, half, block)
                quarter = 0 if by == -1 else 1
                put(e, half, block, quarter, 1, -by, at + quarter).start()

    def gather_rest(e):
        for half in (0, 1):
            for first in (0, -1, 1, 2):
                arrived(e, half, block_at(half, first, 2))

    def send_weight():
        return pltpu.make_async_remote_copy(
            src_ref=weight.at[core], dst_ref=weight.at[core], send_sem=w_send, recv_sem=w_recv,
            device_id=sibling, device_id_type=MESH,
        )

    def send_pair(e):
        return pltpu.make_async_remote_copy(
            src_ref=pair_out.at[e], dst_ref=pair_in.at[e], send_sem=pair_send.at[e], recv_sem=pair_recv.at[e],
            device_id=sibling, device_id_type=MESH,
        )

    def send_ring(e, way, step):
        rows = pl.ds(way * HALF, HALF) if step == 0 else pl.ds(0, HD)
        return pltpu.make_async_remote_copy(
            src_ref=ring_out.at[e, way, step, rows], dst_ref=ring_in.at[e, way, step, rows],
            send_sem=ring_send.at[e, way, step], recv_sem=ring_recv.at[e, way, step],
            device_id=up(1 - 2 * way), device_id_type=MESH,
        )

    def gradient_parts(e):
        @pl.loop(0, 2)
        def _(part):
            blocks = gath[e, pl.ds((1 - core) * DEPTH + part * 4, 4)].reshape(4 * HD, BLOCK)
            pair_out[e, pl.ds(part * 4, 4)] = (
                jnp.dot(blocks, cot[...], preferred_element_type=jnp.float32)
                .astype(jnp.bfloat16).reshape(4, HD, width)
            )
        send_pair(e).start()

        @pl.loop(0, 2)
        def _(part):
            blocks = gath[e, pl.ds(core * DEPTH + part * 4, 4)].reshape(4 * HD, BLOCK)
            kept[e, pl.ds(part * 4, 4)] = jnp.dot(
                blocks, cot[...], preferred_element_type=jnp.float32
            ).reshape(4, HD, width)

    def mix(e):
        @pl.loop(0, ROWS // 4)
        def _(part):
            blocks = gath[e, pl.ds(part * 4, 4)].reshape(4 * HD, BLOCK)
            matrix = weight[lax.div(part, 2), pl.ds(lax.rem(part, 2) * 4, 4), e].reshape(4 * HD, width)
            mixed_sum[...] += lax.dot_general(
                blocks, matrix, (((0,), (0,)), ((), ())), preferred_element_type=jnp.float32
            )

    def ring_start(e):
        send_pair(e).wait_recv()
        for way in (0, 1):
            target = shifted(z, 4, DEPTH)
            rows = pl.ds(way * HALF, HALF)
            ring_out[e, way, 0, rows] = (
                kept[e, target, rows] + pair_in[e, target, rows].astype(jnp.float32)
            ).astype(jnp.bfloat16)
            send_ring(e, way, 0).start()

    def ring_step(e, step):
        for way in (0, 1):
            send_ring(e, way, step - 1).wait_recv()
            target = shifted(z, (4 - step) * (1 - 2 * way), DEPTH)
            for half in (0, 1):
                rows = pl.ds(half * HALF, HALF)
                total = kept[e, target, rows] + pair_in[e, target, rows].astype(jnp.float32)
                if step > 1 or half == way:
                    total += ring_in[e, way, step - 1, rows].astype(jnp.float32)
                ring_out[e, way, step, rows] = total.astype(jnp.bfloat16)
            send_ring(e, way, step).start()

    def ring_end(e):
        send_ring(e, 0, 3).wait_recv()
        send_ring(e, 1, 3).wait_recv()
        total = kept[e, z] + pair_in[e, z].astype(jnp.float32)
        total += ring_in[e, 0, 3].astype(jnp.float32) + ring_in[e, 1, 3].astype(jnp.float32)
        grad_ref[e] = total.astype(jnp.bfloat16)

    kv_own(0)
    kv_own(1)
    for e in range(heads):
        queries[e] = q_ref[:, e * HD:(e + 1) * HD]
    run_max[...] = jnp.full_like(run_max, -1e30)
    run_sum[...] = jnp.zeros_like(run_sum)
    weighted[...] = jnp.zeros_like(weighted)
    mixed_sum[...] = jnp.zeros_like(mixed_sum)
    fetch_weight.wait()
    fetch_cot.wait()
    send_weight().start()

    compute(0, 0)
    kv_pass(0, 1)
    compute(1, 0)
    kv_pass(1, 1)
    compute(0, 1)
    kv_pass(0, 2)
    kv_own(2)
    compute(1, 1)
    kv_pass(1, 2)
    compute(0, 2)
    kv_pass(0, 3)
    compute(2, 0)
    kv_pass(2, 1)
    compute(0, 3)
    kv_pass(0, 4)
    compute(0, 4)
    gather_own(0)
    kv_pass(1, 3)
    compute(1, 2)
    gather_first(0, -1)
    gather_first(0, 1)
    gather_first(0, 2)
    kv_pass(2, 2)
    compute(1, 3)
    kv_pass(1, 4)
    compute(1, 4)
    gather_own(1)
    gather_line(0, 0)
    gather_line(0, -1)
    kv_pass(2, 3)
    compute(2, 1)
    gather_line(0, 1)
    gather_line(0, 2)
    gather_first(1, -1)
    gather_first(1, 1)
    gather_first(1, 2)
    compute(2, 2)
    kv_pass(2, 4)
    gather_rest(0)
    compute(2, 3)
    compute(2, 4)
    gather_own(2)
    gather_line(1, 0)
    gather_line(1, -1)
    gather_line(1, 1)
    gather_line(1, 2)
    gradient_parts(0)
    gather_first(2, -1)
    gather_first(2, 1)
    gather_first(2, 2)
    ring_start(0)
    gather_rest(1)
    gradient_parts(1)
    ring_step(0, 1)
    gather_line(2, 0)
    ring_start(1)
    ring_step(0, 2)
    gather_line(2, -1)
    ring_step(1, 1)
    ring_step(0, 3)
    gather_line(2, 1)
    ring_step(1, 2)
    ring_end(0)
    gather_line(2, 2)
    ring_step(1, 3)
    send_weight().wait_recv()
    mix(0)
    gather_rest(2)
    gradient_parts(2)
    ring_start(2)
    ring_end(1)
    mix(1)
    ring_step(2, 1)
    mix(2)
    ring_step(2, 2)
    mixed_ref[...] = mixed_sum[...].astype(jnp.bfloat16)
    ring_step(2, 3)
    ring_end(2)

    send_weight().wait_send()

    @pl.loop(0, heads)
    def _(e):
        for kind in (is_key, is_value):
            for by in (1, -1):
                for hop in range(4 if (kind == is_key) == (by == 1) else 3):
                    kv(kind, e, shifted(z, -by * hop, DEPTH), by).wait_send()

            @pl.when(core == 0)
            def _():
                @pl.loop(0, DEPTH)
                def _(block):
                    hand(kind, e, block).wait_send()

        for half in (0, 1):
            @pl.loop(0, 11)
            def _(slot):
                put(e, half, me, None, 0, 1, slot).wait_send()

            @pl.loop(11, 19)
            def _(slot):
                put(e, half, me, 0, 0, 1, slot).wait_send()

        send_pair(e).wait_send()
        for way in (0, 1):
            for step in range(4):
                send_ring(e, way, step).wait_send()


def layer(block_mask, queries, keys, values, weight_half, cotangent):
    rows, width = queries.shape
    heads = width // HD
    vmem = pl.BlockSpec(memory_space=pltpu.VMEM)
    anywhere = pl.BlockSpec(memory_space=pl.ANY)
    dma = pltpu.SemaphoreType.DMA
    low, wide = jnp.bfloat16, jnp.float32
    return pl.pallas_call(
        layer_kernel,
        out_shape=(
            jax.ShapeDtypeStruct((rows, width), low),
            jax.ShapeDtypeStruct((heads, HD, width), low),
        ),
        in_specs=[pl.BlockSpec(memory_space=pltpu.SMEM), vmem, vmem, vmem, anywhere, anywhere],
        out_specs=(vmem, vmem),
        scratch_shapes=[
            pltpu.VMEM((heads, BLOCK, HD), low),
            pltpu.VMEM((2, DEPTH, heads, BLOCK, HD), low),
            pltpu.VMEM((2, DEPTH, heads, HD, BLOCK), low),
            pltpu.VMEM((heads, 1, BLOCK), wide),
            pltpu.VMEM((heads, 1, BLOCK), wide),
            pltpu.VMEM((heads, HD, BLOCK), wide),
            pltpu.VMEM((heads, ROWS, HD, BLOCK), low),
            pltpu.VMEM((2, ROWS // 2, heads, HD, width), low),
            pltpu.VMEM((BLOCK, width), low),
            pltpu.VMEM((BLOCK, width), wide),
            pltpu.VMEM((heads, DEPTH, HD, width), wide),
            pltpu.VMEM((heads, DEPTH, HD, width), low),
            pltpu.VMEM((heads, DEPTH, HD, width), low),
            pltpu.VMEM((heads, 2, 4, HD, width), low),
            pltpu.VMEM((heads, 2, 4, HD, width), low),
            dma((2, 2, DEPTH, heads)), dma((2, DEPTH, heads)), dma((2, DEPTH, heads)), dma((2, DEPTH, heads)),
            dma((heads, 2, 19)), dma((heads, 2, ROWS)), dma, dma, dma((2,)),
            dma((heads,)), dma((heads,)), dma((heads, 2, 4)), dma((heads, 2, 4)),
        ],
        compiler_params=pltpu.CompilerParams(
            collective_id=0, has_side_effects=True, vmem_limit_bytes=58 << 20
        ),
    )(block_mask, queries, keys, values, weight_half, cotangent)


def body(queries, keys, values, out_weight, cotangent, block_mask):
    width = queries.shape[1]
    mixed_out, grad_weight = layer(
        block_mask, queries, keys, values, out_weight.reshape(ROWS // 2, width // HD, HD, width), cotangent
    )
    return (mixed_out, grad_weight.reshape(width, width))


def solution(mesh):
    tokens = P(("col", "ctx"), "row")
    return jax.shard_map(
        body,
        mesh=mesh,
        in_specs=(tokens, tokens, tokens, P("col", "row"), tokens, P()),
        out_specs=(tokens, tokens),
        check_vma=False,
    )
```

time: 258 us -> 135 us (0.52)
  waiting for transfers between devices: 99.3 us -> 0 us
  between operations: 14.1 us -> 0.64 us
  local copies, waits for them, and re-layouts: 10.8 us -> 3.49 us
  Pallas kernels: 133 us -> 130 us
    all_gather x2 -> x0, waiting for transfers between devices: 98 us -> none  [the longest x1 51.4 us: body(): all_keys = lax.all_gather(keys, ('col', 'ctx'), axis=0, tiled=True)]
    unnamed x12 -> x2, local copies, waits for them, and re-layouts: 10.8 us -> 3.49 us
    pallas_call x2 -> x1, Pallas kernels: 133 us -> 130 us  [layer(): pl.pallas_call(layer_kernel, out_shape=(jax.ShapeDtypeStruct((rows, width...]
  transfers between devices with their start and end apart: 2 -> 0, of which waited for: 2 -> 0; matrix products, arithmetic and copies ran while one was open for 0% -> 0% of each run, Pallas kernels for 0% -> 0%
where the time goes in v4:
time: 135 us
  Pallas kernels  130 us (96%)
  local copies, waits for them, and re-layouts  3.49 us (3%)
    pallas_call x1, Pallas kernels, layer(): pl.pallas_call(layer_kernel, out_shape=(jax.ShapeDtypeStruct((rows, width...  130 us
    unnamed x2, local copies, waits for them, and re-layouts  3.49 us

profile of v4, /device:TPU:1, one launch (start us, length us, event | category | flops | bytes accessed | tf_op | source)
XLA Modules:
  0.0 134.5 jit_solution(8332539658715271351)
XLA Ops:
  0.6 130.4 %shard_map.77 = (bf16[512,384]{1,0:T(8,128)(2,1)}, bf16[3,128,384]{2,1,0:T(8,128)(2,1)}) custom-call(s32[16,16]{1,0:T(8,128)} %mask_ref.1, bf16[512,384]{1,0:T(8,128)(2,1)} %q_ref.1, bf16[512,384]{1,0:T(8,128)(2,1)} %k_ref.1, bf16[512,384]{1,0:T(8,128)(2,1)} %v_ref.1, bf16[8,3,128,384]{3,2,1,0:T(8,128)(2,1)} %bitcast.2, bf16[512,384]{1,0:T(8,128)(2,1)} %cot_ref.1), custom_call_target="tpu_custom_call" | custom-call | tf_op jit(solution)/shard_map/pallas_call | solution.py:383
  131.0 1.8 %copy.10 = bf16[512,384]{1,0:T(8,128)(2,1)} copy(bf16[512,384]{1,0:T(8,128)(2,1)} %get-tuple-element.8) | data formatting | bytes 786432
  132.8 1.7 %copy.11 = bf16[384,384]{1,0:T(8,128)(2,1)} copy(bf16[384,384]{1,0:T(8,128)(2,1)} %bitcast.3) | data formatting | bytes 589824

commit v5 on v4

--- a/solution.py
+++ b/solution.py
@@ -80,16 +80,16 @@
     def hand_over(kind, e, block):
         pl.when(core == 0)(lambda: hand(kind, e, block).start())
 
-    def kv_own(e):
-        for kind in (is_key, is_value):
+    def kv_own(e, kinds=(0, 1)):
+        for kind in kinds:
             if kind == is_value:
                 values[core, z, e] = v_ref[:, e * HD:(e + 1) * HD].T
             kv(kind, e, z, 1).start()
             kv(kind, e, z, -1).start()
             hand_over(kind, e, z)
 
-    def kv_pass(e, hop):
-        for kind in (is_key, is_value):
+    def kv_pass(e, hop, kinds=(0, 1)):
+        for kind in kinds:
             for by in (1, -1):
                 longer = (kind == is_key) == (by == 1)
                 if hop == 4 and not longer:
@@ -253,7 +253,7 @@
         grad_ref[e] = total.astype(jnp.bfloat16)
 
     kv_own(0)
-    kv_own(1)
+    kv_own(1, (0,))
     for e in range(heads):
         queries[e] = q_ref[:, e * HD:(e + 1) * HD]
     run_max[...] = jnp.full_like(run_max, -1e30)
@@ -266,79 +266,82 @@
 
     compute(0, 0)
     kv_pass(0, 1)
-    compute(1, 0)
-    kv_pass(1, 1)
+    kv_own(1, (1,))
     compute(0, 1)
     kv_pass(0, 2)
-    kv_own(2)
-    compute(1, 1)
-    kv_pass(1, 2)
+    kv_own(2, (0,))
     compute(0, 2)
     kv_pass(0, 3)
-    compute(2, 0)
-    kv_pass(2, 1)
+    kv_pass(1, 1)
+    kv_own(2, (1,))
     compute(0, 3)
     kv_pass(0, 4)
     compute(0, 4)
     gather_own(0)
-    kv_pass(1, 3)
-    compute(1, 2)
+    compute(1, 0)
+    kv_pass(1, 2)
+    kv_pass(2, 1, (0,))
+    compute(1, 1)
     gather_first(0, -1)
     gather_first(0, 1)
     gather_first(0, 2)
-    kv_pass(2, 2)
+    compute(1, 2)
+    gather_line(0, 0)
+    kv_pass(1, 3)
+    kv_pass(2, 1, (1,))
     compute(1, 3)
+    gather_line(0, -1)
+    gather_line(0, 1)
+    gather_line(0, 2)
+    gather_rest(0)
     kv_pass(1, 4)
     compute(1, 4)
     gather_own(1)
-    gather_line(0, 0)
-    gather_line(0, -1)
-    kv_pass(2, 3)
+    kv_pass(2, 2)
+    gradient_parts(0)
+    compute(2, 0)
     compute(2, 1)
-    gather_line(0, 1)
-    gather_line(0, 2)
     gather_first(1, -1)
     gather_first(1, 1)
     gather_first(1, 2)
+    kv_pass(2, 3)
     compute(2, 2)
-    kv_pass(2, 4)
-    gather_rest(0)
     compute(2, 3)
-    compute(2, 4)
-    gather_own(2)
+    ring_start(0)
     gather_line(1, 0)
     gather_line(1, -1)
     gather_line(1, 1)
     gather_line(1, 2)
-    gradient_parts(0)
+    ring_step(0, 1)
+    kv_pass(2, 4)
+    compute(2, 4)
+    gather_own(2)
+    gather_rest(1)
+    gradient_parts(1)
+    ring_step(0, 2)
     gather_first(2, -1)
     gather_first(2, 1)
     gather_first(2, 2)
-    ring_start(0)
-    gather_rest(1)
-    gradient_parts(1)
-    ring_step(0, 1)
+    ring_start(1)
     gather_line(2, 0)
-    ring_start(1)
-    ring_step(0, 2)
     gather_line(2, -1)
-    ring_step(1, 1)
     ring_step(0, 3)
     gather_line(2, 1)
-    ring_step(1, 2)
-    ring_end(0)
     gather_line(2, 2)
-    ring_step(1, 3)
+    ring_step(1, 1)
     send_weight().wait_recv()
-    mix(0)
     gather_rest(2)
     gradient_parts(2)
+    ring_step(1, 2)
     ring_start(2)
+    ring_end(0)
+    mix(0)
+    ring_step(1, 3)
+    ring_step(2, 1)
+    mix(1)
+    ring_step(2, 2)
     ring_end(1)
-    mix(1)
-    ring_step(2, 1)
     mix(2)
-    ring_step(2, 2)
     mixed_ref[...] = mixed_sum[...].astype(jnp.bfloat16)
     ring_step(2, 3)
     ring_end(2)

time: 135 us -> 124 us (0.919)
  Pallas kernels: 130 us -> 119 us
    pallas_call x1, Pallas kernels: 130 us -> 119 us  [layer(): pl.pallas_call(layer_kernel, out_shape=(jax.ShapeDtypeStruct((rows, width...]
where the time goes in v5:
time: 124 us; the launch traced here: 123 us
  Pallas kernels  119 us (96%)
  local copies, waits for them, and re-layouts  3.49 us (3%)
    pallas_call x1, Pallas kernels, layer(): pl.pallas_call(layer_kernel, out_shape=(jax.ShapeDtypeStruct((rows, width...  119 us
    unnamed x2, local copies, waits for them, and re-layouts  3.49 us

profile of v5, /device:TPU:1, one launch (start us, length us, event | category | flops | bytes accessed | tf_op | source)
XLA Modules:
  0.0 123.5 jit_solution(3232039710880311373)
XLA Ops:
  0.6 119.3 %shard_map.77 = (bf16[512,384]{1,0:T(8,128)(2,1)}, bf16[3,128,384]{2,1,0:T(8,128)(2,1)}) custom-call(s32[16,16]{1,0:T(8,128)} %mask_ref.1, bf16[512,384]{1,0:T(8,128)(2,1)} %q_ref.1, bf16[512,384]{1,0:T(8,128)(2,1)} %k_ref.1, bf16[512,384]{1,0:T(8,128)(2,1)} %v_ref.1, bf16[8,3,128,384]{3,2,1,0:T(8,128)(2,1)} %bitcast.2, bf16[512,384]{1,0:T(8,128)(2,1)} %cot_ref.1), custom_call_target="tpu_custom_call" | custom-call | tf_op jit(solution)/shard_map/pallas_call | solution.py:386
  120.0 1.8 %copy.10 = bf16[512,384]{1,0:T(8,128)(2,1)} copy(bf16[512,384]{1,0:T(8,128)(2,1)} %get-tuple-element.8) | data formatting | bytes 786432
  121.8 1.7 %copy.11 = bf16[384,384]{1,0:T(8,128)(2,1)} copy(bf16[384,384]{1,0:T(8,128)(2,1)} %bitcast.3) | data formatting | bytes 589824

commit v6 on v5

--- a/solution.py
+++ b/solution.py
@@ -189,11 +189,11 @@
             device_id=sibling, device_id_type=MESH,
         )
 
-    def send_ring(e, way, step):
-        rows = pl.ds(way * HALF, HALF) if step == 0 else pl.ds(0, HD)
-        return pltpu.make_async_remote_copy(
-            src_ref=ring_out.at[e, way, step, rows], dst_ref=ring_in.at[e, way, step, rows],
-            send_sem=ring_send.at[e, way, step], recv_sem=ring_recv.at[e, way, step],
+    def send_ring(e, way, step, half):
+        ref = pl.ds(half * HALF, HALF)
+        return pltpu.make_async_remote_copy(
+            src_ref=ring_out.at[e, way, step, ref], dst_ref=ring_in.at[e, way, step, ref],
+            send_sem=ring_send.at[e, way, step, half], recv_sem=ring_recv.at[e, way, step, half],
             device_id=up(1 - 2 * way), device_id_type=MESH,
         )
 
@@ -223,31 +223,34 @@
                 blocks, matrix, (((0,), (0,)), ((), ())), preferred_element_type=jnp.float32
             )
 
+    def ring_piece(e, way, step, half):
+        target = shifted(z, (4 - step) * (1 - 2 * way), DEPTH)
+        rows = pl.ds(half * HALF, HALF)
+        total = kept[e, target, rows] + pair_in[e, target, rows].astype(jnp.float32)
+        if step > (0 if half == way else 1):
+            send_ring(e, way, step - 1, half).wait_recv()
+            total += ring_in[e, way, step - 1, rows].astype(jnp.float32)
+        ring_out[e, way, step, rows] = total.astype(jnp.bfloat16)
+        send_ring(e, way, step, half).start()
+
     def ring_start(e):
         send_pair(e).wait_recv()
         for way in (0, 1):
-            target = shifted(z, 4, DEPTH)
-            rows = pl.ds(way * HALF, HALF)
-            ring_out[e, way, 0, rows] = (
-                kept[e, target, rows] + pair_in[e, target, rows].astype(jnp.float32)
-            ).astype(jnp.bfloat16)
-            send_ring(e, way, 0).start()
+            ring_piece(e, way, 0, way)
+        for way in (0, 1):
+            ring_piece(e, way, 1, 1 - way)
 
     def ring_step(e, step):
         for way in (0, 1):
-            send_ring(e, way, step - 1).wait_recv()
-            target = shifted(z, (4 - step) * (1 - 2 * way), DEPTH)
+            ring_piece(e, way, step, way)
+        if step < 3:
+            for way in (0, 1):
+                ring_piece(e, way, step + 1, 1 - way)
+
+    def ring_end(e):
+        for way in (0, 1):
             for half in (0, 1):
-                rows = pl.ds(half * HALF, HALF)
-                total = kept[e, target, rows] + pair_in[e, target, rows].astype(jnp.float32)
-                if step > 1 or half == way:
-                    total += ring_in[e, way, step - 1, rows].astype(jnp.float32)
-                ring_out[e, way, step, rows] = total.astype(jnp.bfloat16)
-            send_ring(e, way, step).start()
-
-    def ring_end(e):
-        send_ring(e, 0, 3).wait_recv()
-        send_ring(e, 1, 3).wait_recv()
+                send_ring(e, way, 3, half).wait_recv()
         total = kept[e, z] + pair_in[e, z].astype(jnp.float32)
         total += ring_in[e, 0, 3].astype(jnp.float32) + ring_in[e, 1, 3].astype(jnp.float32)
         grad_ref[e] = total.astype(jnp.bfloat16)
@@ -286,28 +289,28 @@
     gather_first(0, 1)
     gather_first(0, 2)
     compute(1, 2)
-    gather_line(0, 0)
     kv_pass(1, 3)
     kv_pass(2, 1, (1,))
+    gather_line(0, 0)
+    gather_line(0, -1)
     compute(1, 3)
-    gather_line(0, -1)
     gather_line(0, 1)
     gather_line(0, 2)
-    gather_rest(0)
     kv_pass(1, 4)
     compute(1, 4)
     gather_own(1)
     kv_pass(2, 2)
+    gather_rest(0)
     gradient_parts(0)
     compute(2, 0)
     compute(2, 1)
+    kv_pass(2, 3)
+    ring_start(0)
     gather_first(1, -1)
     gather_first(1, 1)
     gather_first(1, 2)
-    kv_pass(2, 3)
     compute(2, 2)
     compute(2, 3)
-    ring_start(0)
     gather_line(1, 0)
     gather_line(1, -1)
     gather_line(1, 1)
@@ -372,8 +375,9 @@
 
         send_pair(e).wait_send()
         for way in (0, 1):
-            for step in range(4):
-                send_ring(e, way, step).wait_send()
+            for half in (0, 1):
+                for step in range(0 if half == way else 1, 4):
+                    send_ring(e, way, step, half).wait_send()
 
 
 def layer(block_mask, queries, keys, values, weight_half, cotangent):
@@ -409,7 +413,7 @@
             pltpu.VMEM((heads, 2, 4, HD, width), low),
             dma((2, 2, DEPTH, heads)), dma((2, DEPTH, heads)), dma((2, DEPTH, heads)), dma((2, DEPTH, heads)),
             dma((heads, 2, 19)), dma((heads, 2, ROWS)), dma, dma, dma((2,)),
-            dma((heads,)), dma((heads,)), dma((heads, 2, 4)), dma((heads, 2, 4)),
+            dma((heads,)), dma((heads,)), dma((heads, 2, 4, 2)), dma((heads, 2, 4, 2)),
         ],
         compiler_params=pltpu.CompilerParams(
             collective_id=0, has_side_effects=True, vmem_limit_bytes=58 << 20

time: 124 us -> 122 us (0.984)
    pallas_call x1, Pallas kernels: 119 us -> 118 us  [layer(): pl.pallas_call(layer_kernel, out_shape=(jax.ShapeDtypeStruct((rows, width...]
where the time goes in v6:
time: 122 us
  Pallas kernels  118 us (97%)
  local copies, waits for them, and re-layouts  3.49 us (3%)
    pallas_call x1, Pallas kernels, layer(): pl.pallas_call(layer_kernel, out_shape=(jax.ShapeDtypeStruct((rows, width...  118 us
    unnamed x2, local copies, waits for them, and re-layouts  3.49 us

profile of v6, /device:TPU:1, one launch (start us, length us, event | category | flops | bytes accessed | tf_op | source)
XLA Modules:
  0.0 122.0 jit_solution(10675557728577871196)
XLA Ops:
  0.6 117.9 %shard_map.77 = (bf16[512,384]{1,0:T(8,128)(2,1)}, bf16[3,128,384]{2,1,0:T(8,128)(2,1)}) custom-call(s32[16,16]{1,0:T(8,128)} %mask_ref.1, bf16[512,384]{1,0:T(8,128)(2,1)} %q_ref.1, bf16[512,384]{1,0:T(8,128)(2,1)} %k_ref.1, bf16[512,384]{1,0:T(8,128)(2,1)} %v_ref.1, bf16[8,3,128,384]{3,2,1,0:T(8,128)(2,1)} %bitcast.2, bf16[512,384]{1,0:T(8,128)(2,1)} %cot_ref.1), custom_call_target="tpu_custom_call" | custom-call | tf_op jit(solution)/shard_map/pallas_call | solution.py:390
  118.5 1.8 %copy.10 = bf16[512,384]{1,0:T(8,128)(2,1)} copy(bf16[512,384]{1,0:T(8,128)(2,1)} %get-tuple-element.8) | data formatting | bytes 786432
  120.3 1.7 %copy.11 = bf16[384,384]{1,0:T(8,128)(2,1)} copy(bf16[384,384]{1,0:T(8,128)(2,1)} %bitcast.3) | data formatting | bytes 589824

commit v7 on v6

--- a/solution.py
+++ b/solution.py
@@ -254,6 +254,42 @@
         total = kept[e, z] + pair_in[e, z].astype(jnp.float32)
         total += ring_in[e, 0, 3].astype(jnp.float32) + ring_in[e, 1, 3].astype(jnp.float32)
         grad_ref[e] = total.astype(jnp.bfloat16)
+
+    def drain_kv():
+        send_weight().wait_send()
+
+        @pl.loop(0, heads)
+        def _(e):
+            for kind in (is_key, is_value):
+                for by in (1, -1):
+                    for hop in range(4 if (kind == is_key) == (by == 1) else 3):
+                        kv(kind, e, shifted(z, -by * hop, DEPTH), by).wait_send()
+
+                @pl.when(core == 0)
+                def _():
+                    @pl.loop(0, DEPTH)
+                    def _(block):
+                        hand(kind, e, block).wait_send()
+
+    def drain_gather():
+        @pl.loop(0, heads)
+        def _(e):
+            send_pair(e).wait_send()
+            for half in (0, 1):
+                @pl.loop(0, 11)
+                def _(slot):
+                    put(e, half, me, None, 0, 1, slot).wait_send()
+
+                @pl.loop(11, 19)
+                def _(slot):
+                    put(e, half, me, 0, 0, 1, slot).wait_send()
+
+    def drain_ring(e, steps):
+        for way in (0, 1):
+            for half in (0, 1):
+                for step in steps:
+                    if step > 0 or half == way:
+                        send_ring(e, way, step, half).wait_send()
 
     kv_own(0)
     kv_own(1, (0,))
@@ -342,42 +378,18 @@
     ring_step(1, 3)
     ring_step(2, 1)
     mix(1)
+    drain_kv()
     ring_step(2, 2)
     ring_end(1)
     mix(2)
+    drain_gather()
     mixed_ref[...] = mixed_sum[...].astype(jnp.bfloat16)
     ring_step(2, 3)
+    drain_ring(0, range(4))
+    drain_ring(1, range(4))
+    drain_ring(2, range(3))
     ring_end(2)
-
-    send_weight().wait_send()
-
-    @pl.loop(0, heads)
-    def _(e):
-        for kind in (is_key, is_value):
-            for by in (1, -1):
-                for hop in range(4 if (kind == is_key) == (by == 1) else 3):
-                    kv(kind, e, shifted(z, -by * hop, DEPTH), by).wait_send()
-
-            @pl.when(core == 0)
-            def _():
-                @pl.loop(0, DEPTH)
-                def _(block):
-                    hand(kind, e, block).wait_send()
-
-        for half in (0, 1):
-            @pl.loop(0, 11)
-            def _(slot):
-                put(e, half, me, None, 0, 1, slot).wait_send()
-
-            @pl.loop(11, 19)
-            def _(slot):
-                put(e, half, me, 0, 0, 1, slot).wait_send()
-
-        send_pair(e).wait_send()
-        for way in (0, 1):
-            for half in (0, 1):
-                for step in range(0 if half == way else 1, 4):
-                    send_ring(e, way, step, half).wait_send()
+    drain_ring(2, (3,))
 
 
 def layer(block_mask, queries, keys, values, weight_half, cotangent):

time: 122 us -> 122 us (level)
  no operation moved by 1% of the time
where the time goes in v7:
time: 122 us
  Pallas kernels  118 us (97%)
  local copies, waits for them, and re-layouts  3.49 us (3%)
    pallas_call x1, Pallas kernels, layer(): pl.pallas_call(layer_kernel, out_shape=(jax.ShapeDtypeStruct((rows, width...  118 us
    unnamed x2, local copies, waits for them, and re-layouts  3.49 us

profile of v7, /device:TPU:1, one launch (start us, length us, event | category | flops | bytes accessed | tf_op | source)
XLA Modules:
  0.0 121.8 jit_solution(1898312645105672831)
XLA Ops:
  0.6 117.7 %shard_map.77 = (bf16[512,384]{1,0:T(8,128)(2,1)}, bf16[3,128,384]{2,1,0:T(8,128)(2,1)}) custom-call(s32[16,16]{1,0:T(8,128)} %mask_ref.1, bf16[512,384]{1,0:T(8,128)(2,1)} %q_ref.1, bf16[512,384]{1,0:T(8,128)(2,1)} %k_ref.1, bf16[512,384]{1,0:T(8,128)(2,1)} %v_ref.1, bf16[8,3,128,384]{3,2,1,0:T(8,128)(2,1)} %bitcast.2, bf16[512,384]{1,0:T(8,128)(2,1)} %cot_ref.1), custom_call_target="tpu_custom_call" | custom-call | tf_op jit(solution)/shard_map/pallas_call | solution.py:402
  118.3 1.8 %copy.10 = bf16[512,384]{1,0:T(8,128)(2,1)} copy(bf16[512,384]{1,0:T(8,128)(2,1)} %get-tuple-element.8) | data formatting | bytes 786432
  120.1 1.7 %copy.11 = bf16[384,384]{1,0:T(8,128)(2,1)} copy(bf16[384,384]{1,0:T(8,128)(2,1)} %bitcast.3) | data formatting | bytes 589824
